TPU v7x, 256 devices: a whole 4x4x8 slice. The times are simulated.
256 devices in a mesh: seq: 32 (over x, y, core), head: 8 (over z).
Axes of the slice: x: 4, y: 4, z: 8, core: 2. Of those that a mesh axis runs over, the one named last changes fastest.
Arguments:
- queries: bfloat16 [1, 8192, 4096], P(None, 'seq', 'head'), may hold values from -6 to 6
- keys: bfloat16 [1, 8192, 4096], P(None, 'seq', 'head'), may hold values from -6 to 6
- values: bfloat16 [1, 8192, 4096], P(None, 'seq', 'head'), may hold values from -6 to 6
- out_weight: bfloat16 [4096, 4096], P('head'), may hold values from -0.09375 to 0.09375
- out_grad: bfloat16 [1, 8192, 4096], P(None, 'seq', 'head'), may hold values from -6 to 6
- block_doc: int32 [1, 32], replicated, may hold values from 0 to 2, never falling along the last dimension, each value on 1 to 24 neighbouring positions
Outputs:
- context: bfloat16 [1, 8192, 4096], P(None, 'seq', 'head')
- query_grad: bfloat16 [1, 8192, 4096], P(None, 'seq', 'head')
- key_grad: bfloat16 [1, 8192, 4096], P(None, 'seq', 'head')
- value_grad: bfloat16 [1, 8192, 4096], P(None, 'seq', 'head')
- weight_grad: bfloat16 [4096, 4096], P('head', 'seq')
Inputs may be any that keep to these rules, and one draw needn't show every extreme that they name: `block_doc`: document numbers never fall along a pack, every document holds whole leaf blocks, and one document covers exactly 24 blocks.
All inputs are finite; a program needn't handle non-finite values.
Results may differ from a plain program's by a relative error of at most 0.019.
Values may be sent and summed in bfloat16 or wider, within the bound.
No kernel may reach another device: no remote copies, remote signals or barrier semaphores. Data moves between devices by JAX's collectives and lax.ppermute only.
A program may use at most 128 MiB of HBM per device.

v0:
```python
import functools
import math

import jax
import jax.numpy as jnp
from jax import lax
from jax.experimental import pallas as pl
from jax.experimental.pallas import tpu as pltpu
from jax.sharding import PartitionSpec as P

DH = 128
F32 = jnp.float32
BF16 = jnp.bfloat16
HOPS = (1, 2, 6, 8, 24)


def swapped(value, level_num):
    count = lax.axis_size("seq")
    return lax.ppermute(value, "seq", [(i, i ^ HOPS[level_num]) for i in range(count)])


def mm(a, b, dims):
    return lax.dot_general(a, b, (dims, ((), ())), preferred_element_type=F32)


def pool_matrix(rows):
    r = lax.broadcasted_iota(jnp.int32, (rows // 2, rows), 0)
    c = lax.broadcasted_iota(jnp.int32, (rows // 2, rows), 1)
    return jnp.where((c >> 1) == r, 0.5, 0.0).astype(BF16)


def spread_matrix(rows):
    r = lax.broadcasted_iota(jnp.int32, (rows, rows // 2), 0)
    c = lax.broadcasted_iota(jnp.int32, (rows, rows // 2), 1)
    return jnp.where((r >> 1) == c, 0.5, 0.0).astype(BF16)


def pool_into(out_ref, bit, mine, other):
    rows = mine.shape[0]
    half = rows // 2
    mat = pool_matrix(rows)
    low = mm(mat, mine, ((1,), (0,))).astype(BF16)
    high = mm(mat, other, ((1,), (0,))).astype(BF16)
    out_ref[pl.ds(pl.multiple_of(bit * half, half), half), :] = low
    out_ref[pl.ds(pl.multiple_of((1 - bit) * half, half), half), :] = high


def pool_kernel(level_num, place_ref, mine_ref, other_ref, out_ref):
    bit = (place_ref[0] >> level_num) & 1
    pool_into(out_ref, bit, mine_ref[...], other_ref[...])


def pool_first_kernel(place_ref, other_k, other_v, mine_k, mine_v, *out_refs):
    core = place_ref[0] & 1

    def pooled(mine_ref, other_ref):
        width = mine_ref.shape[1] // len(out_refs)
        for i, out_ref in enumerate(out_refs):
            part = slice(i * width, (i + 1) * width)
            pool_into(out_ref, core, mine_ref[:, part], other_ref[:, part])

    pl.when(core == 0)(lambda: pooled(mine_k, other_k))
    pl.when(core == 1)(lambda: pooled(mine_v, other_v))


SMEM = pl.BlockSpec(memory_space=pltpu.SMEM)
VMEM = pl.BlockSpec(memory_space=pltpu.VMEM)


def near_call(kernel, place, near, far, outs, scratch=(), name=None):
    return pl.pallas_call(
        kernel,
        in_specs=[SMEM] + [VMEM] * (len(near) + len(far)),
        out_specs=[VMEM] * len(outs),
        out_shape=[pltpu.VMEM(s, d) if is_near else jax.ShapeDtypeStruct(s, d) for s, d, is_near in outs],
        scratch_shapes=list(scratch),
        name=name,
    )(place, *[pltpu.with_memory_space_constraint(a, pltpu.VMEM) for a in near], *far)


def gather_columns(core, dest_k, dest_v, firsts, mine, other):
    rows = firsts[0].shape[0]
    dest_k[0:rows, :] = firsts[0][...]
    dest_k[rows : 2 * rows, :] = firsts[1][...]
    dest_v[0:rows, :] = firsts[2][...]
    dest_v[rows : 2 * rows, :] = firsts[3][...]

    @pl.when(core == 0)
    def _():
        for i in range(len(mine)):
            dest_k[(2 + i) * rows : (3 + i) * rows, :] = mine[i][...]
            dest_v[(2 + i) * rows : (3 + i) * rows, :] = other[i][...]

    @pl.when(core == 1)
    def _():
        for i in range(len(mine)):
            dest_k[(2 + i) * rows : (3 + i) * rows, :] = other[i][...]
            dest_v[(2 + i) * rows : (3 + i) * rows, :] = mine[i][...]


def forward_kernel(scaling, n_up, place_ref, weight_ref, query_ref, *refs):
    firsts, mine, other = refs[:4], refs[4 : 4 + n_up], refs[4 + n_up : 4 + 2 * n_up]
    context_ref, prob_ref, kcol_ref, vcol_ref = refs[4 + 2 * n_up :]
    gather_columns(place_ref[0] & 1, kcol_ref, vcol_ref, firsts, mine, other)
    col_weight = weight_ref[...]
    scores = mm(query_ref[...], kcol_ref[...], ((1,), (1,))) * scaling
    masked = jnp.where(col_weight > 0.0, scores, -jnp.inf)
    row_max = jnp.max(masked, axis=-1, keepdims=True)
    weights = col_weight * jnp.exp(masked - row_max)
    total = jnp.sum(weights, axis=-1, keepdims=True)
    prob = (weights * (1.0 / total)).astype(BF16)
    prob_ref[0] = prob
    context_ref[...] = mm(prob, vcol_ref[...], ((1,), (0,))).astype(BF16)


def backward_kernel(scaling, n_up, place_ref, query_ref, prob_ref, context_ref, grad_ref, *refs):
    kcol_ref, vcol_ref = refs[:2]
    dq_ref, own_k, own_v, sib_k, sib_v, keep_ref, send_ref = refs[2:]
    core = place_ref[0] & 1
    rows = query_ref.shape[0]
    grad = grad_ref[...]
    prob = prob_ref[0]
    delta = jnp.sum(grad.astype(F32) * context_ref[...].astype(F32), axis=-1, keepdims=True)
    prob_grad = mm(grad, vcol_ref[...], ((1,), (1,)))
    score_grad = (prob.astype(F32) * (prob_grad - delta)).astype(BF16)
    dq_ref[...] = (mm(score_grad, kcol_ref[...], ((1,), (0,))) * scaling).astype(BF16)
    dk = mm(score_grad, query_ref[...], ((0,), (0,))) * scaling
    dv = mm(prob, grad, ((0,), (0,)))
    own_k[...] = dk[:rows]
    own_v[...] = dv[:rows]
    sib_k[...] = dk[rows : 2 * rows]
    sib_v[...] = dv[rows : 2 * rows]
    up_k = dk[2 * rows :].reshape(n_up, rows, DH)
    up_v = dv[2 * rows :].reshape(n_up, rows, DH)

    @pl.when(core == 0)
    def _():
        keep_ref[...] = up_k.astype(BF16)
        send_ref[...] = up_v.astype(BF16)

    @pl.when(core == 1)
    def _():
        keep_ref[...] = up_v.astype(BF16)
        send_ref[...] = up_k.astype(BF16)


def spread_half(hi_ref, lo_ref, bit):
    rows = hi_ref.shape[0]
    half = rows // 2
    mat = spread_matrix(rows)
    part = pl.ds(pl.multiple_of(bit * half, half), half)
    return mm(mat, hi_ref[part, :], ((1,), (0,))) + mm(mat, lo_ref[part, :], ((1,), (0,)))


def split_held(hi_ref, lo_ref, held):
    hi = held.astype(BF16)
    hi_ref[...] = hi
    lo_ref[...] = (held - hi.astype(F32)).astype(BF16)


def top_kernel(place_ref, recv_ref, keep_ref, send_ref, *rest_refs):
    top = keep_ref.shape[0] - 1
    send_ref[...] = (keep_ref[top].astype(F32) + recv_ref[top].astype(F32)).astype(BF16)
    for i, rest_ref in enumerate(rest_refs):
        rest_ref[...] = keep_ref[i].astype(F32) + recv_ref[i].astype(F32)


def climb_kernel(level_num, place_ref, back_ref, rest_ref, *refs):
    held_ref = refs[0] if len(refs) == 5 else None
    send_ref, own_ref, hi_ref, lo_ref = refs[-4:]
    bit = (place_ref[0] >> level_num) & 1
    held = back_ref[...].astype(F32)
    if held_ref is not None:
        held = held + held_ref[...]
    split_held(hi_ref, lo_ref, held)
    other = spread_half(hi_ref, lo_ref, 1 - bit)
    send_ref[...] = (rest_ref[...] + other).astype(BF16)
    own_ref[...] = spread_half(hi_ref, lo_ref, bit)


def leaf_kernel(
    place_ref, back_ref, held_ref, own_k, own_v, sib_k, sib_v,
    send_k, send_v, total_k, total_v, hi_ref, lo_ref,
):
    core = place_ref[0] & 1
    split_held(hi_ref, lo_ref, held_ref[...] + back_ref[...].astype(F32))
    other = spread_half(hi_ref, lo_ref, 1 - core)
    own = spread_half(hi_ref, lo_ref, core)
    zero = jnp.zeros_like(own)
    is_key = core == 0
    send_k[...] = (sib_k[...] + jnp.where(is_key, other, zero)).astype(BF16)
    send_v[...] = (sib_v[...] + jnp.where(is_key, zero, other)).astype(BF16)
    total_k[...] = own_k[...] + jnp.where(is_key, own, zero)
    total_v[...] = own_v[...] + jnp.where(is_key, zero, own)


def context_grad_kernel(offsets, place_ref, depth_ref, weight_ref, *refs):
    count = len(offsets)
    grads, out_ref, send_ref, full_ref = refs[:count], refs[count], refs[count + 1], refs[count + 2]
    acc_ref = refs[count + 3]
    core = place_ref[0] & 1
    width = grads[0].shape[1]
    for i, offset in enumerate(offsets):
        full_ref[(depth_ref[0] + offset) % count] = grads[i][...]
    acc_ref[...] = jnp.zeros_like(acc_ref)

    def add(at, carry):
        acc_ref[...] += mm(full_ref[at], weight_ref[:, pl.ds(pl.multiple_of(at * width, width), width)], ((1,), (1,)))
        for j in range(2):
            cols = pl.ds(pl.multiple_of((2 * j + 1 - core) * DH, DH), DH)
            send_ref[at, :, j * DH : (j + 1) * DH] = full_ref[at, :, cols]
        return carry

    lax.fori_loop(0, count, add, 0)
    out_ref[...] = acc_ref[...].astype(BF16)


def slot_of(distance):
    return jnp.where(distance == 0, 0, jnp.where(distance == 3, 1, distance + 1))


def weight_term_kernel(place_ref, full_ref, other_grads, mine, other, *refs):
    outs, turned_ref, slots = refs[:4], refs[4], refs[5:]
    place = place_ref[0]
    core = place & 1
    rows, width = mine.shape
    part = width // 2
    turned_ref[:, :rows] = mine[...].astype(F32).T.astype(BF16)
    turned_ref[:, rows:] = other[...].astype(F32).T.astype(BF16)

    def term_of(at, carry):
        own = [full_ref[at, :, pl.ds(pl.multiple_of((2 * j + core) * DH, DH), DH)] for j in range(2)]
        own = jnp.concatenate(own, axis=1)
        term = mm(turned_ref[:, :rows], own, ((1,), (0,))) + mm(turned_ref[:, rows:], other_grads[at], ((1,), (0,)))
        term = term.astype(BF16)
        for j in range(2):
            chip = 2 * at + j
            slot_x = slot_of((chip >> 2) ^ (place >> 3))
            slot_y = slot_of((chip & 3) ^ ((place >> 1) & 3))
            slots[0][4 * slot_x + slot_y] = term[:part, j * DH : (j + 1) * DH]
            slots[1][4 * slot_y + slot_x] = term[part:, j * DH : (j + 1) * DH]
        return carry

    lax.fori_loop(0, full_ref.shape[0], term_of, 0)
    half = slots[0].shape[0] // 2
    for i in range(2):
        outs[2 * i][...] = slots[i][half:]
        outs[2 * i + 1][...] = slots[i][:half]


def column_weights(block_doc, my_block, leaf_rows, level_count):
    leaf_iota = jnp.arange(leaf_rows, dtype=jnp.int32)
    block_parts = [
        jnp.full((leaf_rows,), my_block, jnp.int32),
        jnp.full((leaf_rows,), my_block ^ 1, jnp.int32),
    ]
    weight_parts = [jnp.ones((2 * leaf_rows,), F32)]
    for level_num in range(1, level_count):
        group_first = (my_block >> level_num ^ 1) << level_num
        block_parts.append(group_first + leaf_iota // (leaf_rows >> level_num))
        weight_parts.append(jnp.full((leaf_rows,), 2.0**level_num, F32))
    col_block = jnp.concatenate(block_parts)
    col_weight = jnp.concatenate(weight_parts)
    block_ids = jnp.arange(block_doc.shape[1], dtype=jnp.int32)
    col_onehot = (block_ids[:, None] == col_block[None, :]).astype(jnp.int32)
    col_doc = jnp.sum(block_doc[0][:, None] * col_onehot, axis=0)
    own_doc = jnp.sum(block_doc[0] * (block_ids == my_block).astype(jnp.int32))
    return jnp.where(col_doc == own_doc, col_weight, 0.0)[None]


class RingGather:
    def __init__(self, block, axis):
        self.axis, self.count = axis, lax.axis_size(axis)
        self.below, self.above, self.steps = block, block, 0
        self.blocks = [(0, block)]

    def step(self, after):
        count, self.steps = self.count, self.steps + 1
        self.below, self.above, _ = lax.optimization_barrier((self.below, self.above, after))
        self.below = lax.ppermute(self.below, self.axis, [(i, (i + 1) % count) for i in range(count)])
        self.blocks.append((-self.steps % count, self.below))
        if self.steps < count - self.steps:
            self.above = lax.ppermute(self.above, self.axis, [(i, (i - 1) % count) for i in range(count)])
            self.blocks.append((self.steps, self.above))


N_PARTS = 1


def local(queries, keys, values, out_weight, out_grad, block_doc):
    seq_count = lax.axis_size("seq")
    level_count = seq_count.bit_length() - 1
    n_up = level_count - 1
    my_block = lax.axis_index("seq")
    place = my_block.astype(jnp.int32)[None]
    depth = lax.axis_index("head").astype(jnp.int32)[None]
    _, rows, features = queries.shape
    heads = features // DH
    part_heads = heads // N_PARTS
    part_width = part_heads * DH
    cols = (level_count + 1) * rows
    scaling = 1.0 / math.sqrt(DH)
    queries, keys, values = queries[0], keys[0], values[0]
    tall = (rows, part_width)

    other_keys = swapped(keys, 0)
    other_values = swapped(values, 0)
    ring = RingGather(out_grad[0], "head")
    ring.step(other_values)
    chains = list(
        near_call(
            pool_first_kernel,
            place,
            (other_keys, other_values),
            (keys, values),
            [(tall, BF16, True)] * N_PARTS,
            name="pool_leaf",
        )
    )
    mine, other = [[] for _ in chains], [[] for _ in chains]
    for level_num in range(1, level_count):
        for i in range(N_PARTS):
            got = swapped(chains[i], level_num)
            mine[i].append(got)
            other[i].append(swapped(got, 0))
            if level_num + 1 < level_count:
                (chains[i],) = near_call(
                    functools.partial(pool_kernel, level_num),
                    place,
                    (chains[i], got),
                    (),
                    [(tall, BF16, True)],
                    name="pool_group",
                )
        if level_num + 1 < level_count:
            ring.step(mine[0][-1])
    offsets = tuple(o for o, _ in ring.blocks)
    full_grad = [b for _, b in ring.blocks]
    col_weight = column_weights(block_doc, my_block, rows, level_count)
    out_weight = after(out_weight, mine[0][-1])
    context_grad, send_grad, stacked_grad = pl.pallas_call(
        functools.partial(context_grad_kernel, offsets),
        in_specs=[SMEM, SMEM] + [VMEM] * (1 + len(offsets)),
        out_specs=[VMEM, VMEM, VMEM],
        out_shape=[
            jax.ShapeDtypeStruct((rows, features), BF16),
            jax.ShapeDtypeStruct((len(offsets), rows, features // 2), BF16),
            jax.ShapeDtypeStruct((len(offsets), rows, features), BF16),
        ],
        scratch_shapes=[pltpu.VMEM((rows, features), F32)],
        name="context_grad",
    )(place, depth, out_weight, *full_grad)
    other_grad = swapped(send_grad, 0)

    slab = pl.BlockSpec((rows, DH), lambda h: (0, h))
    col_slab = pl.BlockSpec((cols, DH), lambda h: (0, h))
    prob_slab = pl.BlockSpec((1, rows, cols), lambda h: (h, 0, 0))
    up_slab = pl.BlockSpec((n_up, rows, DH), lambda h: (0, 0, h))
    whole_slabs = [
        pl.BlockSpec((rows, DH), functools.partial(lambda first, h: (0, first + h), i * part_heads))
        for i in range(N_PARTS)
    ]
    forward = []
    for i in range(N_PARTS):
        forward.append(
            pl.pallas_call(
                functools.partial(forward_kernel, scaling, n_up),
                grid=(part_heads,),
                in_specs=[SMEM, pl.BlockSpec((1, cols), lambda h: (0, 0))]
                + [whole_slabs[i]] * 5
                + [slab] * (2 * n_up),
                out_specs=[slab, prob_slab, col_slab, col_slab],
                out_shape=[
                    jax.ShapeDtypeStruct(tall, BF16),
                    jax.ShapeDtypeStruct((part_heads, rows, cols), BF16),
                    jax.ShapeDtypeStruct((cols, part_width), BF16),
                    jax.ShapeDtypeStruct((cols, part_width), BF16),
                ],
                name="attention_forward",
            )(place, col_weight, queries, keys, other_keys, values, other_values, *mine[i], *other[i])
        )
    contexts = [f[0] for f in forward]
    (context,) = contexts
    shape = (seq_count // 4, features // 2, DH)
    weight_outs = pl.pallas_call(
        weight_term_kernel,
        in_specs=[SMEM] + [VMEM] * 4,
        out_specs=[VMEM] * 4,
        out_shape=[jax.ShapeDtypeStruct(shape, BF16)] * 4,
        scratch_shapes=[pltpu.VMEM((features, 2 * rows), BF16)]
        + [pltpu.VMEM((seq_count // 2, features // 2, DH), BF16)] * 2,
        name="weight_term",
    )(place, stacked_grad, other_grad, context, swapped(context, 0))
    weight_parts = [
        HalvedSum(weight_outs[0], weight_outs[1], (3, 4, 1, 2)),
        HalvedSum(weight_outs[2], weight_outs[3], (1, 2, 3, 4)),
    ]
    context_grad = after(context_grad, *[w.send for w in weight_parts])
    partial_grads = []
    for i in range(N_PARTS):
        context, prob, kcols, vcols = forward[i]
        partial_grads.append(
            pl.pallas_call(
                functools.partial(backward_kernel, scaling, n_up),
                grid=(part_heads,),
                in_specs=[SMEM, whole_slabs[i], prob_slab, slab, whole_slabs[i], col_slab, col_slab],
                out_specs=[slab] * 5 + [up_slab, up_slab],
                out_shape=[jax.ShapeDtypeStruct(tall, BF16)]
                + [jax.ShapeDtypeStruct(tall, F32)] * 4
                + [
                    jax.ShapeDtypeStruct((n_up,) + tall, BF16),
                    jax.ShapeDtypeStruct((n_up,) + tall, BF16),
                ],
                name="attention_backward",
            )(place, queries, prob, context, context_grad, kcols, vcols)
        )
    query_grad = jnp.concatenate([g[0] for g in partial_grads], axis=1)
    halves = [pltpu.VMEM(tall, BF16), pltpu.VMEM(tall, BF16)]
    keep = [g[5] for g in partial_grads]
    recv_up = [swapped(g[6], 0) for g in partial_grads]
    back, held, rest = [None] * N_PARTS, [None] * N_PARTS, [None] * N_PARTS
    for i in range(N_PARTS):
        send, *rest[i] = near_call(
            top_kernel,
            place,
            (recv_up[i],),
            (keep[i],),
            [(tall, BF16, True)] + [(tall, F32, False)] * (n_up - 1),
            name="hand_down_top",
        )
        back[i] = swapped(send, level_count - 1)
    for level_num in range(level_count - 2, 0, -1):
        for w in weight_parts:
            w.step()
        for i in range(N_PARTS):
            back[i] = after(back[i], *[w.send for w in weight_parts])
            send, held[i] = near_call(
                functools.partial(climb_kernel, level_num),
                place,
                (back[i],),
                (rest[i][level_num - 1],) + (() if held[i] is None else (held[i],)),
                [(tall, BF16, True), (tall, F32, False)],
                scratch=halves,
                name="hand_down",
            )
            back[i] = swapped(send, level_num)
    for w in weight_parts:
        w.step()
    weight_grad = jnp.concatenate([w.keep for w in weight_parts], axis=0)
    key_grads, value_grads = [], []
    for i in range(N_PARTS):
        send_k, send_v, total_k, total_v = near_call(
            leaf_kernel,
            place,
            (back[i],),
            (held[i],) + tuple(partial_grads[i][1:5]),
            [(tall, BF16, True), (tall, BF16, True), (tall, F32, False), (tall, F32, False)],
            scratch=halves,
            name="hand_down_leaf",
        )
        key_grads.append((total_k + swapped(send_k, 0).astype(F32)).astype(BF16))
        value_grads.append((total_v + swapped(send_v, 0).astype(F32)).astype(BF16))
    context = jnp.concatenate(contexts, axis=1)
    key_grad = jnp.concatenate(key_grads, axis=1)
    value_grad = jnp.concatenate(value_grads, axis=1)
    return context[None], query_grad[None], key_grad[None], value_grad[None], weight_grad


def after(value, *others):
    return lax.optimization_barrier((value,) + others)[0]


class HalvedSum:
    def __init__(self, send, keep, level_nums):
        self.send, self.keep, self.levels = send, keep, list(level_nums)

    def step(self):
        got = swapped(self.send, self.levels.pop(0))
        half = self.keep.shape[0] // 2
        if not self.levels:
            self.keep = (self.keep[0].astype(F32) + got[0].astype(F32)).astype(BF16)
            return
        self.send = (self.keep[half:].astype(F32) + got[half:].astype(F32)).astype(BF16)
        self.keep = self.keep[:half].astype(F32) + got[:half].astype(F32)


def solution(mesh):
    placed = (
        P(None, "seq", "head"),
        P(None, "seq", "head"),
        P(None, "seq", "head"),
        P("head", None),
        P(None, "seq", "head"),
        P(),
    )
    return jax.shard_map(
        local,
        mesh=mesh,
        in_specs=placed,
        out_specs=(
            P(None, "seq", "head"),
            P(None, "seq", "head"),
            P(None, "seq", "head"),
            P(None, "seq", "head"),
            P("head", "seq"),
        ),
        check_vma=False,
    )
```

profile of v0, /device:TPU:1, one launch (start us, length us, event | category | flops | bytes accessed | tf_op | source)
XLA Modules:
  0.0 151.4 jit_solution(2479693826150601371)
XLA Ops:
  0.6 3.3 %collective-permute-start.1 = (bf16[256,512]{1,0:T(8,128)(2,1)}, bf16[256,512]{1,0:T(8,128)(2,1)S(1)}, u32[]{:S(2)}, u32[]{:S(2)}) collective-permute-start(bf16[256,512]{1,0:T(8,128)(2,1)} %bitcast.24), channel_id=1, source_target_pairs={{0,8},{8,0},{16,24},{24,16},{32,40},{40,32},{48,56},{56,48},{64,72... | collective-permute-start | bytes 786440 | tf_op jit(solution)/shard_map/ppermute | solution.py:19
  8.4 3.9 %collective-permute-start.11 = (bf16[256,512]{1,0:T(8,128)(2,1)}, bf16[256,512]{1,0:T(8,128)(2,1)S(1)}, u32[]{:S(2)}, u32[]{:S(2)}) collective-permute-start(bf16[256,512]{1,0:T(8,128)(2,1)} %bitcast.28), channel_id=1, source_target_pairs={{0,7},{1,0},{2,1},{3,2},{4,3},{5,4},{6,5},{7,6},{8,15},{9,8},{10,9... | collective-permute-start | bytes 786440 | tf_op jit(solution)/shard_map/ppermute | solution.py:283
  16.0 2.6 %collective-permute-done.10.refs_1_ = bf16[256,512]{1,0:T(8,128)(2,1)S(1)} collective-permute-done((bf16[256,512]{1,0:T(8,128)(2,1)}, bf16[256,512]{1,0:T(8,128)(2,1)S(1)}, u32[]{:S(2)}, u32[]{:S(2)}) %collective-permute-start.10) | collective-permute-done | bytes 262176 | tf_op jit(solution)/shard_map/ppermute | solution.py:280
  18.6 3.1 %collective-permute-start.13 = (bf16[256,512]{1,0:T(8,128)(2,1)S(1)}, bf16[256,512]{1,0:T(8,128)(2,1)S(1)}, u32[]{:S(2)}, u32[]{:S(2)}) collective-permute-start(bf16[256,512]{1,0:T(8,128)(2,1)S(1)} %collective-permute-done.11.refs_2_), channel_id=1, source_target_pairs={{0,7},{1,0},{2,1},{3,2},{4,3},{5,4},{6,5},{7,6},{8,15},{9,8},{10,9... | collective-permute-start | bytes 786440 | tf_op jit(solution)/shard_map/ppermute | solution.py:283
  23.3 3.5 %collective-permute-done.12.refs_3_ = bf16[256,512]{1,0:T(8,128)(2,1)S(1)} collective-permute-done((bf16[256,512]{1,0:T(8,128)(2,1)S(1)}, bf16[256,512]{1,0:T(8,128)(2,1)S(1)}, u32[]{:S(2)}, u32[]{:S(2)}) %collective-permute-start.12) | collective-permute-done | bytes 262176 | tf_op jit(solution)/shard_map/ppermute | solution.py:280
  29.5 4.2 %collective-permute-done.14.refs_5_ = bf16[256,512]{1,0:T(8,128)(2,1)S(1)} collective-permute-done((bf16[256,512]{1,0:T(8,128)(2,1)S(1)}, bf16[256,512]{1,0:T(8,128)(2,1)S(1)}, u32[]{:S(2)}, u32[]{:S(2)}) %collective-permute-start.14) | collective-permute-done | bytes 262176 | tf_op jit(solution)/shard_map/ppermute | solution.py:280
  35.4 2.6 %collective-permute-start.5 = (bf16[256,512]{1,0:T(8,128)(2,1)S(1)}, bf16[256,512]{1,0:T(8,128)(2,1)S(1)}, u32[]{:S(2)}, u32[]{:S(2)}) collective-permute-start(bf16[256,512]{1,0:T(8,128)(2,1)S(1)} %pool_group.5), channel_id=1, source_target_pairs={{0,192},{8,200},{16,208},{24,216},{32,224},{40,232},{48,240},{56,2... | collective-permute-start | bytes 786440 | tf_op jit(solution)/shard_map/ppermute | solution.py:19
  38.0 4.3 %collective-permute-done.5.refs_7_ = bf16[256,512]{1,0:T(8,128)(2,1)S(1)} collective-permute-done((bf16[256,512]{1,0:T(8,128)(2,1)S(1)}, bf16[256,512]{1,0:T(8,128)(2,1)S(1)}, u32[]{:S(2)}, u32[]{:S(2)}) %collective-permute-start.5) | collective-permute-done | bytes 262176 | tf_op jit(solution)/shard_map/ppermute | solution.py:19
  42.4 7.2 %context_grad.1 = (bf16[256,512]{1,0:T(8,128)(2,1)}, bf16[8,256,256]{2,1,0:T(8,128)(2,1)}, bf16[8,256,512]{2,1,0:T(8,128)(2,1)}) custom-call(s32[1]{0:T(128)} %bitcast.place_ref, s32[1]{0:T(128)} %bitcast.6.depth_ref, bf16[512,4096]{1,0:T(8,128)(2,1)} %weight_ref, bf16[256,512]{1,0:T(8,128)(2,1)} %bitcast.29, bf16[256,512]{1,0:T(8,128)(2,1)} %copy-done.14, ...), custom_call_target="tpu_custom_call" | custom-call | tf_op jit(solution)/shard_map/context_grad/pallas_call | solution.py:341
  49.6 4.7 %collective-permute-start.17 = (bf16[8,256,256]{2,1,0:T(8,128)(2,1)}, bf16[8,256,256]{2,1,0:T(8,128)(2,1)S(1)}, u32[]{:S(2)}, u32[]{:S(2)}) collective-permute-start(bf16[8,256,256]{2,1,0:T(8,128)(2,1)} %get-tuple-element.61), channel_id=1, source_target_pairs={{0,8},{8,0},{16,24},{24,16},{32,40},{40,32},{48,56},{56,48},{64,72... | collective-permute-start | bytes 3145736 | tf_op jit(solution)/shard_map/ppermute | solution.py:19
  58.7 7.2 %attention_forward.1 = (bf16[256,512]{1,0:T(8,128)(2,1)}, bf16[4,256,1536]{2,1,0:T(8,128)(2,1)}, bf16[1536,512]{1,0:T(8,128)(2,1)}, bf16[1536,512]{1,0:T(8,128)(2,1)}) custom-call(s32[1]{0:T(128)} %bitcast.place_ref, f32[1,1536]{1,0:T(1,128)} %select_n.33.weight_ref, bf16[256,512]{1,0:T(8,128)(2,1)} %bitcast.18, bf16[256,512]{1,0:T(8,128)(2,1)} %bitcast.23, ...), custom_call_target="tpu_custom_call" | custom-call | tf_op jit(solution)/shard_map/attention_forward/pallas_call | solution.py:366
  68.8 6.1 %weight_term.1 = (bf16[8,256,128]{2,1,0:T(8,128)(2,1)}, bf16[8,256,128]{2,1,0:T(8,128)(2,1)}, bf16[8,256,128]{2,1,0:T(8,128)(2,1)}, bf16[8,256,128]{2,1,0:T(8,128)(2,1)}) custom-call(s32[1]{0:T(128)} %bitcast.place_ref, bf16[8,256,512]{2,1,0:T(8,128)(2,1)} %get-tuple-element.60.full_ref, bf16[8,256,256]{2,1,0:T(8,128)(2,1)} %copy-done.5, ...), custom_call_target="tpu_custom_call" | custom-call | tf_op jit(solution)/shard_map/weight_term/pallas_call | solution.py:385
  74.9 7.7 %attention_backward.1 = (bf16[256,512]{1,0:T(8,128)(2,1)}, f32[256,512]{1,0:T(8,128)}, f32[256,512]{1,0:T(8,128)}, f32[256,512]{1,0:T(8,128)}, f32[256,512]{1,0:...) custom-call(s32[1]{0:T(128)} %bitcast.place_ref, bf16[256,512]{1,0:T(8,128)(2,1)} %bitcast.19, ...), custom_call_target="tpu_custom_call" | custom-call | tf_op jit(solution)/shard_map/attention_backward/pallas_call | solution.py:403
  83.1 13.4 %collective-permute-done.21 = bf16[8,256,128]{2,1,0:T(8,128)(2,1)S(1)} collective-permute-done((bf16[8,256,128]{2,1,0:T(8,128)(2,1)S(1)}, bf16[8,256,128]{2,1,0:T(8,128)(2,1)S(1)}, u32[]{:S(2)}, u32[]{:S(2)}) %collective-permute-start.21) | collective-permute-done | bytes 524320 | tf_op jit(solution)/shard_map/ppermute | solution.py:19
  97.3 2.5 %collective-permute-start.24 = (bf16[4,256,128]{2,1,0:T(8,128)(2,1)}, bf16[4,256,128]{2,1,0:T(8,128)(2,1)}, u32[]{:S(2)}, u32[]{:S(2)}) collective-permute-start(bf16[4,256,128]{2,1,0:T(8,128)(2,1)} %get-tuple-element.96), channel_id=1, source_target_pairs={{0,192},{8,200},{16,208},{24,216},{32,224},{40,232},{48,240},{56,2... | collective-permute-start | bytes 786440 | tf_op jit(solution)/shard_map/ppermute | solution.py:19
  99.8 2.5 %hand_down_top.1 = (bf16[256,512]{1,0:T(8,128)(2,1)S(1)}, f32[256,512]{1,0:T(8,128)}, f32[256,512]{1,0:T(8,128)}, f32[256,512]{1,0:T(8,128)}) custom-call(s32[1]{0:T(128)} %bitcast.place_ref, bf16[4,256,512]{2,1,0:T(8,128)(2,1)S(1)} %collective-permute-done.19.recv_ref, bf16[4,256,512]{2,1,0:T(8,128)(2,1)} %get-tuple-element.69.keep_ref), custom_call_target="tpu_custom_call" | custom-call | tf_op jit(solution)/shard_map/hand_down_top/pallas_call | solution.py:71
  104.0 7.7 %collective-permute-done.20.back_ref = bf16[256,512]{1,0:T(8,128)(2,1)S(1)} collective-permute-done((bf16[256,512]{1,0:T(8,128)(2,1)S(1)}, bf16[256,512]{1,0:T(8,128)(2,1)S(1)}, u32[]{:S(2)}, u32[]{:S(2)}) %collective-permute-start.20) | collective-permute-done | bytes 262176 | tf_op jit(solution)/shard_map/ppermute | solution.py:19
  116.9 3.8 %collective-permute-done.23.back_ref = bf16[256,512]{1,0:T(8,128)(2,1)S(1)} collective-permute-done((bf16[256,512]{1,0:T(8,128)(2,1)S(1)}, bf16[256,512]{1,0:T(8,128)(2,1)S(1)}, u32[]{:S(2)}, u32[]{:S(2)}) %collective-permute-start.23) | collective-permute-done | bytes 262176 | tf_op jit(solution)/shard_map/ppermute | solution.py:19
  120.7 2.5 %hand_down.4 = (bf16[256,512]{1,0:T(8,128)(2,1)S(1)}, f32[256,512]{1,0:T(8,128)}) custom-call(s32[1]{0:T(128)} %bitcast.place_ref, bf16[256,512]{1,0:T(8,128)(2,1)S(1)} %collective-permute-done.23.back_ref, f32[256,512]{1,0:T(8,128)} %get-tuple-element.77.rest_ref, f32[256,512]{1,0:T(8,128)} %get-tuple-element.78.refs_0_), custom_call_target="tpu_custom_call" | custom-call | tf_op jit(solution)/shard_map/hand_down/pallas_call | solution.py:71
  126.0 3.6 %collective-permute-done.26.back_ref = bf16[256,512]{1,0:T(8,128)(2,1)S(1)} collective-permute-done((bf16[256,512]{1,0:T(8,128)(2,1)S(1)}, bf16[256,512]{1,0:T(8,128)(2,1)S(1)}, u32[]{:S(2)}, u32[]{:S(2)}) %collective-permute-start.26) | collective-permute-done | bytes 262176 | tf_op jit(solution)/shard_map/ppermute | solution.py:19
  129.7 2.6 %hand_down.5 = (bf16[256,512]{1,0:T(8,128)(2,1)S(1)}, f32[256,512]{1,0:T(8,128)}) custom-call(s32[1]{0:T(128)} %bitcast.place_ref, bf16[256,512]{1,0:T(8,128)(2,1)S(1)} %collective-permute-done.26.back_ref, f32[256,512]{1,0:T(8,128)} %get-tuple-element.81.rest_ref, f32[256,512]{1,0:T(8,128)} %get-tuple-element.82.refs_0_), custom_call_target="tpu_custom_call" | custom-call | tf_op jit(solution)/shard_map/hand_down/pallas_call | solution.py:71
  133.6 3.9 %collective-permute-done.29.back_ref = bf16[256,512]{1,0:T(8,128)(2,1)S(1)} collective-permute-done((bf16[256,512]{1,0:T(8,128)(2,1)S(1)}, bf16[256,512]{1,0:T(8,128)(2,1)S(1)}, u32[]{:S(2)}, u32[]{:S(2)}) %collective-permute-start.29) | collective-permute-done | bytes 262176 | tf_op jit(solution)/shard_map/ppermute | solution.py:19
  137.4 3.2 %hand_down_leaf.1 = (bf16[256,512]{1,0:T(8,128)(2,1)S(1)}, bf16[256,512]{1,0:T(8,128)(2,1)S(1)}, f32[256,512]{1,0:T(8,128)}, f32[256,512]{1,0:T(8,128)}) custom-call(s32[1]{0:T(128)} %bitcast.place_ref, bf16[256,512]{1,0:T(8,128)(2,1)S(1)} %collective-permute-done.29.back_ref, f32[256,512]{1,0:T(8,128)} %get-tuple-element.84.held_ref, ...), custom_call_target="tpu_custom_call" | custom-call | tf_op jit(solution)/shard_map/hand_down_leaf/pallas_call | solution.py:71
  140.7 5.9 %collective-permute-start.31 = (bf16[256,512]{1,0:T(8,128)(2,1)S(1)}, bf16[256,512]{1,0:T(8,128)(2,1)S(1)}, u32[]{:S(2)}, u32[]{:S(2)}) collective-permute-start(bf16[256,512]{1,0:T(8,128)(2,1)S(1)} %get-tuple-element.92), channel_id=1, source_target_pairs={{0,8},{8,0},{16,24},{24,16},{32,40},{40,32},{48,56},{56,48},{64,72... | collective-permute-start | bytes 786440 | tf_op jit(solution)/shard_map/ppermute | solution.py:19
  (125 shorter events, 38.6 us)
Async XLA Ops:
  7.1 7.6 %collective-permute-start.2 = (bf16[256,512]{1,0:T(8,128)(2,1)S(1)}, bf16[256,512]{1,0:T(8,128)(2,1)S(1)}, u32[]{:S(2)}, u32[]{:S(2)}) collective-permute-start(bf16[256,512]{1,0:T(8,128)(2,1)S(1)} %pool_leaf.1.mine_ref), channel_id=1, source_target_pairs={{0,16},{8,24},{16,0},{24,8},{32,48},{40,56},{48,32},{56,40},{64,80... | collective-permute-start | bytes 786440 | tf_op jit(solution)/shard_map/ppermute | solution.py:19
  7.2 11.4 %collective-permute-start.10 = (bf16[256,512]{1,0:T(8,128)(2,1)}, bf16[256,512]{1,0:T(8,128)(2,1)S(1)}, u32[]{:S(2)}, u32[]{:S(2)}) collective-permute-start(bf16[256,512]{1,0:T(8,128)(2,1)} %bitcast.27), channel_id=1, source_target_pairs={{0,1},{1,2},{2,3},{3,4},{4,5},{5,6},{6,7},{7,0},{8,9},{9,10},{10,1... | collective-permute-start | bytes 786440 | tf_op jit(solution)/shard_map/ppermute | solution.py:280
  8.4 10.2 %collective-permute-start.11 = (bf16[256,512]{1,0:T(8,128)(2,1)}, bf16[256,512]{1,0:T(8,128)(2,1)S(1)}, u32[]{:S(2)}, u32[]{:S(2)}) collective-permute-start(bf16[256,512]{1,0:T(8,128)(2,1)} %bitcast.28), channel_id=1, source_target_pairs={{0,7},{1,0},{2,1},{3,2},{4,3},{5,4},{6,5},{7,6},{8,15},{9,8},{10,9... | collective-permute-start | bytes 786440 | tf_op jit(solution)/shard_map/ppermute | solution.py:283
  14.9 7.9 %collective-permute-start.3 = (bf16[256,512]{1,0:T(8,128)(2,1)S(1)}, bf16[256,512]{1,0:T(8,128)(2,1)S(1)}, u32[]{:S(2)}, u32[]{:S(2)}) collective-permute-start(bf16[256,512]{1,0:T(8,128)(2,1)S(1)} %pool_group.3.mine_ref), channel_id=1, source_target_pairs={{0,48},{8,56},{16,32},{24,40},{32,16},{40,24},{48,0},{56,8},{64,11... | collective-permute-start | bytes 786440 | tf_op jit(solution)/shard_map/ppermute | solution.py:19
  18.6 8.2 %collective-permute-start.12 = (bf16[256,512]{1,0:T(8,128)(2,1)S(1)}, bf16[256,512]{1,0:T(8,128)(2,1)S(1)}, u32[]{:S(2)}, u32[]{:S(2)}) collective-permute-start(bf16[256,512]{1,0:T(8,128)(2,1)S(1)} %collective-permute-done.10.refs_1_), channel_id=1, source_target_pairs={{0,1},{1,2},{2,3},{3,4},{4,5},{5,6},{6,7},{7,0},{8,9},{9,10},{10,1... | collective-permute-start | bytes 786440 | tf_op jit(solution)/shard_map/ppermute | solution.py:280
  18.6 8.1 %collective-permute-start.13 = (bf16[256,512]{1,0:T(8,128)(2,1)S(1)}, bf16[256,512]{1,0:T(8,128)(2,1)S(1)}, u32[]{:S(2)}, u32[]{:S(2)}) collective-permute-start(bf16[256,512]{1,0:T(8,128)(2,1)S(1)} %collective-permute-done.11.refs_2_), channel_id=1, source_target_pairs={{0,7},{1,0},{2,1},{3,2},{4,3},{5,4},{6,5},{7,6},{8,15},{9,8},{10,9... | collective-permute-start | bytes 786440 | tf_op jit(solution)/shard_map/ppermute | solution.py:283
  23.0 6.5 %collective-permute-start.4 = (bf16[256,512]{1,0:T(8,128)(2,1)S(1)}, bf16[256,512]{1,0:T(8,128)(2,1)S(1)}, u32[]{:S(2)}, u32[]{:S(2)}) collective-permute-start(bf16[256,512]{1,0:T(8,128)(2,1)S(1)} %pool_group.4.mine_ref), channel_id=1, source_target_pairs={{0,64},{8,72},{16,80},{24,88},{32,96},{40,104},{48,112},{56,120},{... | collective-permute-start | bytes 786440 | tf_op jit(solution)/shard_map/ppermute | solution.py:19
  26.8 6.9 %collective-permute-start.14 = (bf16[256,512]{1,0:T(8,128)(2,1)S(1)}, bf16[256,512]{1,0:T(8,128)(2,1)S(1)}, u32[]{:S(2)}, u32[]{:S(2)}) collective-permute-start(bf16[256,512]{1,0:T(8,128)(2,1)S(1)} %collective-permute-done.12.refs_3_), channel_id=1, source_target_pairs={{0,1},{1,2},{2,3},{3,4},{4,5},{5,6},{6,7},{7,0},{8,9},{9,10},{10,1... | collective-permute-start | bytes 786440 | tf_op jit(solution)/shard_map/ppermute | solution.py:280
  27.3 6.5 %collective-permute-start.15 = (bf16[256,512]{1,0:T(8,128)(2,1)S(1)}, bf16[256,512]{1,0:T(8,128)(2,1)S(1)}, u32[]{:S(2)}, u32[]{:S(2)}) collective-permute-start(bf16[256,512]{1,0:T(8,128)(2,1)S(1)} %collective-permute-done.13.refs_4_), channel_id=1, source_target_pairs={{0,7},{1,0},{2,1},{3,2},{4,3},{5,4},{6,5},{7,6},{8,15},{9,8},{10,9... | collective-permute-start | bytes 786440 | tf_op jit(solution)/shard_map/ppermute | solution.py:283
  33.7 8.6 %collective-permute-start.16 = (bf16[256,512]{1,0:T(8,128)(2,1)S(1)}, bf16[256,512]{1,0:T(8,128)(2,1)}, u32[]{:S(2)}, u32[]{:S(2)}) collective-permute-start(bf16[256,512]{1,0:T(8,128)(2,1)S(1)} %collective-permute-done.14.refs_5_), channel_id=1, source_target_pairs={{0,1},{1,2},{2,3},{3,4},{4,5},{5,6},{6,7},{7,0},{8,9},{9,10},{10,1... | collective-permute-start | bytes 786440 | tf_op jit(solution)/shard_map/ppermute | solution.py:280
  35.4 6.9 %collective-permute-start.5 = (bf16[256,512]{1,0:T(8,128)(2,1)S(1)}, bf16[256,512]{1,0:T(8,128)(2,1)S(1)}, u32[]{:S(2)}, u32[]{:S(2)}) collective-permute-start(bf16[256,512]{1,0:T(8,128)(2,1)S(1)} %pool_group.5), channel_id=1, source_target_pairs={{0,192},{8,200},{16,208},{24,216},{32,224},{40,232},{48,240},{56,2... | collective-permute-start | bytes 786440 | tf_op jit(solution)/shard_map/ppermute | solution.py:19
  49.6 18.2 %collective-permute-start.17 = (bf16[8,256,256]{2,1,0:T(8,128)(2,1)}, bf16[8,256,256]{2,1,0:T(8,128)(2,1)S(1)}, u32[]{:S(2)}, u32[]{:S(2)}) collective-permute-start(bf16[8,256,256]{2,1,0:T(8,128)(2,1)} %get-tuple-element.61), channel_id=1, source_target_pairs={{0,8},{8,0},{16,24},{24,16},{32,40},{40,32},{48,56},{56,48},{64,72... | collective-permute-start | bytes 3145736 | tf_op jit(solution)/shard_map/ppermute | solution.py:19
  82.7 17.1 %collective-permute-start.19 = (bf16[4,256,512]{2,1,0:T(8,128)(2,1)}, bf16[4,256,512]{2,1,0:T(8,128)(2,1)S(1)}, u32[]{:S(2)}, u32[]{:S(2)}) collective-permute-start(bf16[4,256,512]{2,1,0:T(8,128)(2,1)} %get-tuple-element.68), channel_id=1, source_target_pairs={{0,8},{8,0},{16,24},{24,16},{32,40},{40,32},{48,56},{56,48},{64,72... | collective-permute-start | bytes 3145736 | tf_op jit(solution)/shard_map/ppermute | solution.py:19
  83.1 13.4 %collective-permute-start.21 = (bf16[8,256,128]{2,1,0:T(8,128)(2,1)S(1)}, bf16[8,256,128]{2,1,0:T(8,128)(2,1)S(1)}, u32[]{:S(2)}, u32[]{:S(2)}) collective-permute-start(bf16[8,256,128]{2,1,0:T(8,128)(2,1)S(1)} %copy-done.22), channel_id=1, source_target_pairs={{0,64},{8,72},{16,80},{24,88},{32,96},{40,104},{48,112},{56,120},{... | collective-permute-start | bytes 1572872 | tf_op jit(solution)/shard_map/ppermute | solution.py:19
  83.1 19.4 %collective-permute-start.22 = (bf16[8,256,128]{2,1,0:T(8,128)(2,1)}, bf16[8,256,128]{2,1,0:T(8,128)(2,1)S(1)}, u32[]{:S(2)}, u32[]{:S(2)}) collective-permute-start(bf16[8,256,128]{2,1,0:T(8,128)(2,1)} %get-tuple-element.63), channel_id=1, source_target_pairs={{0,16},{8,24},{16,0},{24,8},{32,48},{40,56},{48,32},{56,40},{64,80... | collective-permute-start | bytes 1572872 | tf_op jit(solution)/shard_map/ppermute | solution.py:19
  97.3 16.9 %collective-permute-start.24 = (bf16[4,256,128]{2,1,0:T(8,128)(2,1)}, bf16[4,256,128]{2,1,0:T(8,128)(2,1)}, u32[]{:S(2)}, u32[]{:S(2)}) collective-permute-start(bf16[4,256,128]{2,1,0:T(8,128)(2,1)} %get-tuple-element.96), channel_id=1, source_target_pairs={{0,192},{8,200},{16,208},{24,216},{32,224},{40,232},{48,240},{56,2... | collective-permute-start | bytes 786440 | tf_op jit(solution)/shard_map/ppermute | solution.py:19
  102.3 9.5 %collective-permute-start.20 = (bf16[256,512]{1,0:T(8,128)(2,1)S(1)}, bf16[256,512]{1,0:T(8,128)(2,1)S(1)}, u32[]{:S(2)}, u32[]{:S(2)}) collective-permute-start(bf16[256,512]{1,0:T(8,128)(2,1)S(1)} %get-tuple-element.70), channel_id=1, source_target_pairs={{0,192},{8,200},{16,208},{24,216},{32,224},{40,232},{48,240},{56,2... | collective-permute-start | bytes 786440 | tf_op jit(solution)/shard_map/ppermute | solution.py:19
  102.6 12.7 %collective-permute-start.25 = (bf16[4,256,128]{2,1,0:T(8,128)(2,1)S(1)}, bf16[4,256,128]{2,1,0:T(8,128)(2,1)S(1)}, u32[]{:S(2)}, u32[]{:S(2)}) collective-permute-start(bf16[4,256,128]{2,1,0:T(8,128)(2,1)S(1)} %get-tuple-element.94), channel_id=1, source_target_pairs={{0,48},{8,56},{16,32},{24,40},{32,16},{40,24},{48,0},{56,8},{64,11... | collective-permute-start | bytes 786440 | tf_op jit(solution)/shard_map/ppermute | solution.py:19
  114.2 6.5 %collective-permute-start.23 = (bf16[256,512]{1,0:T(8,128)(2,1)S(1)}, bf16[256,512]{1,0:T(8,128)(2,1)S(1)}, u32[]{:S(2)}, u32[]{:S(2)}) collective-permute-start(bf16[256,512]{1,0:T(8,128)(2,1)S(1)} %get-tuple-element.75), channel_id=1, source_target_pairs={{0,64},{8,72},{16,80},{24,88},{32,96},{40,104},{48,112},{56,120},{... | collective-permute-start | bytes 786440 | tf_op jit(solution)/shard_map/ppermute | solution.py:19
  115.2 9.4 %collective-permute-start.27 = (bf16[2,256,128]{2,1,0:T(8,128)(2,1)S(1)}, bf16[2,256,128]{2,1,0:T(8,128)(2,1)S(1)}, u32[]{:S(2)}, u32[]{:S(2)}) collective-permute-start(bf16[2,256,128]{2,1,0:T(8,128)(2,1)S(1)} %get-tuple-element.100), channel_id=1, source_target_pairs={{0,16},{8,24},{16,0},{24,8},{32,48},{40,56},{48,32},{56,40},{64,80... | collective-permute-start | bytes 393224 | tf_op jit(solution)/shard_map/ppermute | solution.py:19
  115.4 10.6 %collective-permute-start.28 = (bf16[2,256,128]{2,1,0:T(8,128)(2,1)S(1)}, bf16[2,256,128]{2,1,0:T(8,128)(2,1)S(1)}, u32[]{:S(2)}, u32[]{:S(2)}) collective-permute-start(bf16[2,256,128]{2,1,0:T(8,128)(2,1)S(1)} %get-tuple-element.98), channel_id=1, source_target_pairs={{0,64},{8,72},{16,80},{24,88},{32,96},{40,104},{48,112},{56,120},{... | collective-permute-start | bytes 393224 | tf_op jit(solution)/shard_map/ppermute | solution.py:19
  124.6 8.9 %collective-permute-start.32 = (bf16[1,256,128]{2,1,0:T(8,128)(2,1)S(1)}, bf16[1,256,128]{2,1,0:T(8,128)(2,1)S(1)}, u32[]{:S(2)}, u32[]{:S(2)}) collective-permute-start(bf16[1,256,128]{2,1,0:T(8,128)(2,1)S(1)} %fusion.9), channel_id=1, source_target_pairs={{0,48},{8,56},{16,32},{24,40},{32,16},{40,24},{48,0},{56,8},{64,11... | collective-permute-start | bytes 196616 | tf_op jit(solution)/shard_map/ppermute | solution.py:19
  132.2 14.4 %collective-permute-start.33 = (bf16[1,256,128]{2,1,0:T(8,128)(2,1)S(1)}, bf16[1,256,128]{2,1,0:T(8,128)(2,1)S(1)}, u32[]{:S(2)}, u32[]{:S(2)}) collective-permute-start(bf16[1,256,128]{2,1,0:T(8,128)(2,1)S(1)} %fusion.8), channel_id=1, source_target_pairs={{0,192},{8,200},{16,208},{24,216},{32,224},{40,232},{48,240},{56,2... | collective-permute-start | bytes 196616 | tf_op jit(solution)/shard_map/ppermute | solution.py:19
  140.7 7.1 %collective-permute-start.31 = (bf16[256,512]{1,0:T(8,128)(2,1)S(1)}, bf16[256,512]{1,0:T(8,128)(2,1)S(1)}, u32[]{:S(2)}, u32[]{:S(2)}) collective-permute-start(bf16[256,512]{1,0:T(8,128)(2,1)S(1)} %get-tuple-element.92), channel_id=1, source_target_pairs={{0,8},{8,0},{16,24},{24,16},{32,40},{40,32},{48,56},{56,48},{64,72... | collective-permute-start | bytes 786440 | tf_op jit(solution)/shard_map/ppermute | solution.py:19
  (33 other events, 408.0 us)
where the time goes:
time: 152 us; the launch traced here: 151 us
  waiting for transfers between devices  54.4 us (36%)
  Pallas kernels  43.4 us (29%)
  starting transfers between devices  42.5 us (28%)
  other arithmetic  7.82 us (5%)
  local copies, waits for them, and re-layouts  2.43 us (2%)
    ppermute x27, waiting for transfers between devices, swapped(): lax.ppermute(value, 'seq', [(i, i ^ HOPS[level_num]) for i in range(count)])  44.1 us
    ppermute x27, starting transfers between devices, swapped(): lax.ppermute(value, 'seq', [(i, i ^ HOPS[level_num]) for i in range(count)])  30 us
    pallas_call x9, Pallas kernels, near_call(): pl.pallas_call(kernel, in_specs=[SMEM] + [VMEM] * (len(near) + len(far)),...  15.2 us
    ppermute x4, waiting for transfers between devices, step(): lax.ppermute(self.below, self.axis, [(i, (i + 1) % count) for i in range(...  10.2 us
    ppermute x3, starting transfers between devices, step(): lax.ppermute(self.above, self.axis, [(i, (i - 1) % count) for i in range(...  9.3 us
    pallas_call x1, Pallas kernels, local(): pl.pallas_call(functools.partial(backward_kernel, scaling, n_up), grid=(p...  7.73 us
    pallas_call x1, Pallas kernels, local(): pl.pallas_call(functools.partial(forward_kernel, scaling, n_up), grid=(pa...  7.2 us
    pallas_call x1, Pallas kernels, local(): pl.pallas_call(functools.partial(context_grad_kernel, offsets), in_specs=...  7.19 us
  transfers between devices with their start and end apart: 34, of which 17 were waited for; matrix products, arithmetic and copies ran while one was open for 4% of the time, Pallas kernels for 14%

commit v1 on v0

--- a/solution.py
+++ b/solution.py
@@ -126,10 +126,10 @@
     dq_ref[...] = (mm(score_grad, kcol_ref[...], ((1,), (0,))) * scaling).astype(BF16)
     dk = mm(score_grad, query_ref[...], ((0,), (0,))) * scaling
     dv = mm(prob, grad, ((0,), (0,)))
-    own_k[...] = dk[:rows]
-    own_v[...] = dv[:rows]
-    sib_k[...] = dk[rows : 2 * rows]
-    sib_v[...] = dv[rows : 2 * rows]
+    own_k[...] = dk[:rows].astype(BF16)
+    own_v[...] = dv[:rows].astype(BF16)
+    sib_k[...] = dk[rows : 2 * rows].astype(BF16)
+    sib_v[...] = dv[rows : 2 * rows].astype(BF16)
     up_k = dk[2 * rows :].reshape(n_up, rows, DH)
     up_v = dv[2 * rows :].reshape(n_up, rows, DH)
 
@@ -162,7 +162,7 @@
     top = keep_ref.shape[0] - 1
     send_ref[...] = (keep_ref[top].astype(F32) + recv_ref[top].astype(F32)).astype(BF16)
     for i, rest_ref in enumerate(rest_refs):
-        rest_ref[...] = keep_ref[i].astype(F32) + recv_ref[i].astype(F32)
+        rest_ref[...] = (keep_ref[i].astype(F32) + recv_ref[i].astype(F32)).astype(BF16)
 
 
 def climb_kernel(level_num, place_ref, back_ref, rest_ref, *refs):
@@ -174,7 +174,7 @@
         held = held + held_ref[...]
     split_held(hi_ref, lo_ref, held)
     other = spread_half(hi_ref, lo_ref, 1 - bit)
-    send_ref[...] = (rest_ref[...] + other).astype(BF16)
+    send_ref[...] = (rest_ref[...].astype(F32) + other).astype(BF16)
     own_ref[...] = spread_half(hi_ref, lo_ref, bit)
 
 
@@ -188,31 +188,28 @@
     own = spread_half(hi_ref, lo_ref, core)
     zero = jnp.zeros_like(own)
     is_key = core == 0
-    send_k[...] = (sib_k[...] + jnp.where(is_key, other, zero)).astype(BF16)
-    send_v[...] = (sib_v[...] + jnp.where(is_key, zero, other)).astype(BF16)
-    total_k[...] = own_k[...] + jnp.where(is_key, own, zero)
-    total_v[...] = own_v[...] + jnp.where(is_key, zero, own)
+    send_k[...] = (sib_k[...].astype(F32) + jnp.where(is_key, other, zero)).astype(BF16)
+    send_v[...] = (sib_v[...].astype(F32) + jnp.where(is_key, zero, other)).astype(BF16)
+    total_k[...] = own_k[...].astype(F32) + jnp.where(is_key, own, zero)
+    total_v[...] = own_v[...].astype(F32) + jnp.where(is_key, zero, own)
 
 
 def context_grad_kernel(offsets, place_ref, depth_ref, weight_ref, *refs):
     count = len(offsets)
     grads, out_ref, send_ref, full_ref = refs[:count], refs[count], refs[count + 1], refs[count + 2]
-    acc_ref = refs[count + 3]
     core = place_ref[0] & 1
     width = grads[0].shape[1]
+    total = None
     for i, offset in enumerate(offsets):
-        full_ref[(depth_ref[0] + offset) % count] = grads[i][...]
-    acc_ref[...] = jnp.zeros_like(acc_ref)
-
-    def add(at, carry):
-        acc_ref[...] += mm(full_ref[at], weight_ref[:, pl.ds(pl.multiple_of(at * width, width), width)], ((1,), (1,)))
+        at = (depth_ref[0] + offset) % count
+        block = grads[i][...]
+        full_ref[at] = block
         for j in range(2):
             cols = pl.ds(pl.multiple_of((2 * j + 1 - core) * DH, DH), DH)
-            send_ref[at, :, j * DH : (j + 1) * DH] = full_ref[at, :, cols]
-        return carry
-
-    lax.fori_loop(0, count, add, 0)
-    out_ref[...] = acc_ref[...].astype(BF16)
+            send_ref[at, :, j * DH : (j + 1) * DH] = grads[i][:, cols]
+        part = mm(block, weight_ref[:, pl.ds(pl.multiple_of(at * width, width), width)], ((1,), (1,)))
+        total = part if total is None else total + part
+    out_ref[...] = total.astype(BF16)
 
 
 def slot_of(distance):
@@ -333,7 +330,7 @@
                     name="pool_group",
                 )
         if level_num + 1 < level_count:
-            ring.step(mine[0][-1])
+            ring.step(chains[0])
     offsets = tuple(o for o, _ in ring.blocks)
     full_grad = [b for _, b in ring.blocks]
     col_weight = column_weights(block_doc, my_block, rows, level_count)
@@ -347,7 +344,6 @@
             jax.ShapeDtypeStruct((len(offsets), rows, features // 2), BF16),
             jax.ShapeDtypeStruct((len(offsets), rows, features), BF16),
         ],
-        scratch_shapes=[pltpu.VMEM((rows, features), F32)],
         name="context_grad",
     )(place, depth, out_weight, *full_grad)
     other_grad = swapped(send_grad, 0)
@@ -406,7 +402,7 @@
                 in_specs=[SMEM, whole_slabs[i], prob_slab, slab, whole_slabs[i], col_slab, col_slab],
                 out_specs=[slab] * 5 + [up_slab, up_slab],
                 out_shape=[jax.ShapeDtypeStruct(tall, BF16)]
-                + [jax.ShapeDtypeStruct(tall, F32)] * 4
+                + [jax.ShapeDtypeStruct(tall, BF16)] * 4
                 + [
                     jax.ShapeDtypeStruct((n_up,) + tall, BF16),
                     jax.ShapeDtypeStruct((n_up,) + tall, BF16),
@@ -425,15 +421,19 @@
             place,
             (recv_up[i],),
             (keep[i],),
-            [(tall, BF16, True)] + [(tall, F32, False)] * (n_up - 1),
+            [(tall, BF16, True)] + [(tall, BF16, False)] * (n_up - 1),
             name="hand_down_top",
         )
         back[i] = swapped(send, level_count - 1)
+        for w in weight_parts:
+            w.keep = after(w.keep, send)
     for level_num in range(level_count - 2, 0, -1):
-        for w in weight_parts:
-            w.step()
+        if level_num < level_count - 2:
+            for w in weight_parts:
+                w.step()
         for i in range(N_PARTS):
-            back[i] = after(back[i], *[w.send for w in weight_parts])
+            if level_num < level_count - 2:
+                back[i] = after(back[i], *[w.send for w in weight_parts])
             send, held[i] = near_call(
                 functools.partial(climb_kernel, level_num),
                 place,
@@ -446,6 +446,9 @@
             back[i] = swapped(send, level_num)
     for w in weight_parts:
         w.step()
+    back[-1] = after(back[-1], *[w.send for w in weight_parts])
+    for w in weight_parts:
+        w.step()
     weight_grad = jnp.concatenate([w.keep for w in weight_parts], axis=0)
     key_grads, value_grads = [], []
     for i in range(N_PARTS):
@@ -454,7 +457,7 @@
             place,
             (back[i],),
             (held[i],) + tuple(partial_grads[i][1:5]),
-            [(tall, BF16, True), (tall, BF16, True), (tall, F32, False), (tall, F32, False)],
+            [(tall, BF16, True), (tall, BF16, True), (tall, F32, True), (tall, F32, True)],
             scratch=halves,
             name="hand_down_leaf",
         )

time: 152 us -> 133 us (0.88)
  waiting for transfers between devices: 54.4 us -> 36.4 us
  starting transfers between devices: 42.5 us -> 47 us
  Pallas kernels: 43.4 us -> 40.1 us
  other arithmetic: 7.82 us -> 5.08 us
    ppermute x27, waiting for transfers between devices: 44.1 us -> 25.2 us  [swapped(): lax.ppermute(value, 'seq', [(i, i ^ HOPS[level_num]) for i in range(count)])]
    ppermute x27, starting transfers between devices: 30 us -> 34.6 us  [swapped(): lax.ppermute(value, 'seq', [(i, i ^ HOPS[level_num]) for i in range(count)])]
    pallas_call x9, Pallas kernels: 15.2 us -> 13.5 us  [near_call(): pl.pallas_call(kernel, in_specs=[SMEM] + [VMEM] * (len(near) + len(far)),...]
  transfers between devices with their start and end apart: 34 -> 34, of which waited for: 17 -> 19; matrix products, arithmetic and copies ran while one was open for 4% -> 4% of each run, Pallas kernels for 14% -> 15%
where the time goes in v1:
time: 133 us
  starting transfers between devices  47 us (35%)
  Pallas kernels  40.1 us (30%)
  waiting for transfers between devices  36.4 us (27%)
  other arithmetic  5.08 us (4%)
  local copies, waits for them, and re-layouts  3.11 us (2%)
    ppermute x27, starting transfers between devices, swapped(): lax.ppermute(value, 'seq', [(i, i ^ HOPS[level_num]) for i in range(count)])  34.6 us
    ppermute x27, waiting for transfers between devices, swapped(): lax.ppermute(value, 'seq', [(i, i ^ HOPS[level_num]) for i in range(count)])  25.2 us
    pallas_call x9, Pallas kernels, near_call(): pl.pallas_call(kernel, in_specs=[SMEM] + [VMEM] * (len(near) + len(far)),...  13.5 us
    ppermute x4, waiting for transfers between devices, step(): lax.ppermute(self.below, self.axis, [(i, (i + 1) % count) for i in range(...  11.2 us
    ppermute x3, starting transfers between devices, step(): lax.ppermute(self.above, self.axis, [(i, (i - 1) % count) for i in range(...  9.3 us
    pallas_call x1, Pallas kernels, local(): pl.pallas_call(functools.partial(backward_kernel, scaling, n_up), grid=(p...  7.46 us
    pallas_call x1, Pallas kernels, local(): pl.pallas_call(functools.partial(forward_kernel, scaling, n_up), grid=(pa...  7.18 us
    pallas_call x1, Pallas kernels, local(): pl.pallas_call(weight_term_kernel, in_specs=[SMEM] + [VMEM] * 4, out_spec...  6.02 us
  transfers between devices with their start and end apart: 34, of which 19 were waited for; matrix products, arithmetic and copies ran while one was open for 4% of the time, Pallas kernels for 15%

profile of v1, /device:TPU:1, one launch (start us, length us, event | category | flops | bytes accessed | tf_op | source)
XLA Modules:
  0.0 132.6 jit_solution(15275437982456020021)
XLA Ops:
  0.6 3.3 %collective-permute-start = (bf16[256,512]{1,0:T(8,128)(2,1)}, bf16[256,512]{1,0:T(8,128)(2,1)S(1)}, u32[]{:S(2)}, u32[]{:S(2)}) collective-permute-start(bf16[256,512]{1,0:T(8,128)(2,1)} %bitcast.21), channel_id=1, source_target_pairs={{0,8},{8,0},{16,24},{24,16},{32,40},{40,32},{48,56},{56,48},{64,72... | collective-permute-start | bytes 786440 | tf_op jit(solution)/shard_map/ppermute | solution.py:19
  8.4 3.9 %collective-permute-start.11 = (bf16[256,512]{1,0:T(8,128)(2,1)}, bf16[256,512]{1,0:T(8,128)(2,1)S(1)}, u32[]{:S(2)}, u32[]{:S(2)}) collective-permute-start(bf16[256,512]{1,0:T(8,128)(2,1)} %bitcast.28), channel_id=1, source_target_pairs={{0,7},{1,0},{2,1},{3,2},{4,3},{5,4},{6,5},{7,6},{8,15},{9,8},{10,9... | collective-permute-start | bytes 786440 | tf_op jit(solution)/shard_map/ppermute | solution.py:280
  12.3 2.4 %collective-permute-done.2.other_ref.refs_4_ = bf16[256,512]{1,0:T(8,128)(2,1)S(1)} collective-permute-done((bf16[256,512]{1,0:T(8,128)(2,1)S(1)}, bf16[256,512]{1,0:T(8,128)(2,1)S(1)}, u32[]{:S(2)}, u32[]{:S(2)}) %collective-permute-start.2) | collective-permute-done | bytes 262176 | tf_op jit(solution)/shard_map/ppermute | solution.py:19
  16.0 2.6 %collective-permute-done.10.refs_1_ = bf16[256,512]{1,0:T(8,128)(2,1)S(1)} collective-permute-done((bf16[256,512]{1,0:T(8,128)(2,1)}, bf16[256,512]{1,0:T(8,128)(2,1)S(1)}, u32[]{:S(2)}, u32[]{:S(2)}) %collective-permute-start.10) | collective-permute-done | bytes 262176 | tf_op jit(solution)/shard_map/ppermute | solution.py:277
  18.6 3.1 %collective-permute-start.13 = (bf16[256,512]{1,0:T(8,128)(2,1)S(1)}, bf16[256,512]{1,0:T(8,128)(2,1)S(1)}, u32[]{:S(2)}, u32[]{:S(2)}) collective-permute-start(bf16[256,512]{1,0:T(8,128)(2,1)S(1)} %collective-permute-done.11.refs_2_), channel_id=1, source_target_pairs={{0,7},{1,0},{2,1},{3,2},{4,3},{5,4},{6,5},{7,6},{8,15},{9,8},{10,9... | collective-permute-start | bytes 786440 | tf_op jit(solution)/shard_map/ppermute | solution.py:280
  23.3 3.5 %collective-permute-done.12.refs_3_ = bf16[256,512]{1,0:T(8,128)(2,1)S(1)} collective-permute-done((bf16[256,512]{1,0:T(8,128)(2,1)S(1)}, bf16[256,512]{1,0:T(8,128)(2,1)S(1)}, u32[]{:S(2)}, u32[]{:S(2)}) %collective-permute-start.12) | collective-permute-done | bytes 262176 | tf_op jit(solution)/shard_map/ppermute | solution.py:277
  27.3 2.3 %collective-permute-start.15 = (bf16[256,512]{1,0:T(8,128)(2,1)S(1)}, bf16[256,512]{1,0:T(8,128)(2,1)}, u32[]{:S(2)}, u32[]{:S(2)}) collective-permute-start(bf16[256,512]{1,0:T(8,128)(2,1)S(1)} %collective-permute-done.13.refs_4_), channel_id=1, source_target_pairs={{0,7},{1,0},{2,1},{3,2},{4,3},{5,4},{6,5},{7,6},{8,15},{9,8},{10,9... | collective-permute-start | bytes 786440 | tf_op jit(solution)/shard_map/ppermute | solution.py:280
  29.8 2.6 %collective-permute-start.5 = (bf16[256,512]{1,0:T(8,128)(2,1)S(1)}, bf16[256,512]{1,0:T(8,128)(2,1)S(1)}, u32[]{:S(2)}, u32[]{:S(2)}) collective-permute-start(bf16[256,512]{1,0:T(8,128)(2,1)S(1)} %pool_group.5), channel_id=1, source_target_pairs={{0,192},{8,200},{16,208},{24,216},{32,224},{40,232},{48,240},{56,2... | collective-permute-start | bytes 786440 | tf_op jit(solution)/shard_map/ppermute | solution.py:19
  36.4 3.8 %collective-permute-done.16.refs_7_ = bf16[256,512]{1,0:T(8,128)(2,1)S(1)} collective-permute-done((bf16[256,512]{1,0:T(8,128)(2,1)S(1)}, bf16[256,512]{1,0:T(8,128)(2,1)S(1)}, u32[]{:S(2)}, u32[]{:S(2)}) %collective-permute-start.16) | collective-permute-done | bytes 262176 | tf_op jit(solution)/shard_map/ppermute | solution.py:277
  40.9 5.9 %context_grad.1 = (bf16[256,512]{1,0:T(8,128)(2,1)}, bf16[8,256,256]{2,1,0:T(8,128)(2,1)}, bf16[8,256,512]{2,1,0:T(8,128)(2,1)}) custom-call(s32[1]{0:T(128)} %bitcast.place_ref, s32[1]{0:T(128)} %bitcast.6.depth_ref, bf16[512,4096]{1,0:T(8,128)(2,1)} %weight_ref, bf16[256,512]{1,0:T(8,128)(2,1)} %bitcast.29, bf16[256,512]{1,0:T(8,128)(2,1)} %copy-done.14, ...), custom_call_target="tpu_custom_call" | custom-call | tf_op jit(solution)/shard_map/context_grad/pallas_call | solution.py:338
  46.8 4.3 %collective-permute-start.17 = (bf16[8,256,256]{2,1,0:T(8,128)(2,1)}, bf16[8,256,256]{2,1,0:T(8,128)(2,1)S(1)}, u32[]{:S(2)}, u32[]{:S(2)}) collective-permute-start(bf16[8,256,256]{2,1,0:T(8,128)(2,1)} %get-tuple-element.63), channel_id=1, source_target_pairs={{0,8},{8,0},{16,24},{24,16},{32,40},{40,32},{48,56},{56,48},{64,72... | collective-permute-start | bytes 3145736 | tf_op jit(solution)/shard_map/ppermute | solution.py:19
  55.6 7.2 %attention_forward.1 = (bf16[256,512]{1,0:T(8,128)(2,1)}, bf16[4,256,1536]{2,1,0:T(8,128)(2,1)}, bf16[1536,512]{1,0:T(8,128)(2,1)}, bf16[1536,512]{1,0:T(8,128)(2,1)}) custom-call(s32[1]{0:T(128)} %bitcast.place_ref, f32[1,1536]{1,0:T(1,128)} %select_n.33.weight_ref, bf16[256,512]{1,0:T(8,128)(2,1)} %bitcast.18, bf16[256,512]{1,0:T(8,128)(2,1)} %bitcast.23, ...), custom_call_target="tpu_custom_call" | custom-call | tf_op jit(solution)/shard_map/attention_forward/pallas_call | solution.py:362
  65.7 6.0 %weight_term.1 = (bf16[8,256,128]{2,1,0:T(8,128)(2,1)}, bf16[8,256,128]{2,1,0:T(8,128)(2,1)}, bf16[8,256,128]{2,1,0:T(8,128)(2,1)}, bf16[8,256,128]{2,1,0:T(8,128)(2,1)}) custom-call(s32[1]{0:T(128)} %bitcast.place_ref, bf16[8,256,512]{2,1,0:T(8,128)(2,1)} %get-tuple-element.62.full_ref, bf16[8,256,256]{2,1,0:T(8,128)(2,1)} %copy-done.5, ...), custom_call_target="tpu_custom_call" | custom-call | tf_op jit(solution)/shard_map/weight_term/pallas_call | solution.py:381
  71.7 7.5 %attention_backward.1 = (bf16[256,512]{1,0:T(8,128)(2,1)}, bf16[256,512]{1,0:T(8,128)(2,1)}, bf16[256,512]{1,0:T(8,128)(2,1)}, bf16[256,512]{1,0:T(8,128)(2,1)},...) custom-call(s32[1]{0:T(128)} %bitcast.place_ref, bf16[256,512]{1,0:T(8,128)(2,1)} %bitcast.19, ...), custom_call_target="tpu_custom_call" | custom-call | tf_op jit(solution)/shard_map/attention_backward/pallas_call | solution.py:399
  82.2 2.2 %hand_down_top.1 = (bf16[256,512]{1,0:T(8,128)(2,1)S(1)}, bf16[256,512]{1,0:T(8,128)(2,1)}, bf16[256,512]{1,0:T(8,128)(2,1)}, bf16[256,512]{1,0:T(8,128)(2,1)}) custom-call(s32[1]{0:T(128)} %bitcast.place_ref, bf16[4,256,512]{2,1,0:T(8,128)(2,1)S(1)} %collective-permute-done.19.recv_ref, bf16[4,256,512]{2,1,0:T(8,128)(2,1)} %get-tuple-element.71.keep_ref), custom_call_target="tpu_custom_call" | custom-call | tf_op jit(solution)/shard_map/hand_down_top/pallas_call | solution.py:71
  84.4 2.5 %collective-permute-start.20 = (bf16[256,512]{1,0:T(8,128)(2,1)S(1)}, bf16[256,512]{1,0:T(8,128)(2,1)S(1)}, u32[]{:S(2)}, u32[]{:S(2)}) collective-permute-start(bf16[256,512]{1,0:T(8,128)(2,1)S(1)} %get-tuple-element.72), channel_id=1, source_target_pairs={{0,192},{8,200},{16,208},{24,216},{32,224},{40,232},{48,240},{56,2... | collective-permute-start | bytes 786440 | tf_op jit(solution)/shard_map/ppermute | solution.py:19
  86.9 6.4 %collective-permute-done.23 = bf16[8,256,128]{2,1,0:T(8,128)(2,1)} collective-permute-done((bf16[8,256,128]{2,1,0:T(8,128)(2,1)}, bf16[8,256,128]{2,1,0:T(8,128)(2,1)}, u32[]{:S(2)}, u32[]{:S(2)}) %collective-permute-start.23) | collective-permute-done | bytes 524320 | tf_op jit(solution)/shard_map/ppermute | solution.py:19
  96.4 2.3 %hand_down.3 = (bf16[256,512]{1,0:T(8,128)(2,1)S(1)}, f32[256,512]{1,0:T(8,128)}) custom-call(s32[1]{0:T(128)} %bitcast.place_ref, bf16[256,512]{1,0:T(8,128)(2,1)S(1)} %collective-permute-done.20.back_ref, bf16[256,512]{1,0:T(8,128)(2,1)} %get-tuple-element.73.rest_ref), custom_call_target="tpu_custom_call" | custom-call | tf_op jit(solution)/shard_map/hand_down/pallas_call | solution.py:71
  105.3 2.5 %hand_down.4 = (bf16[256,512]{1,0:T(8,128)(2,1)S(1)}, f32[256,512]{1,0:T(8,128)}) custom-call(s32[1]{0:T(128)} %bitcast.place_ref, bf16[256,512]{1,0:T(8,128)(2,1)S(1)} %collective-permute-done.21.back_ref, bf16[256,512]{1,0:T(8,128)(2,1)} %get-tuple-element.80.rest_ref, f32[256,512]{1,0:T(8,128)} %get-tuple-element.81.refs_0_), custom_call_target="tpu_custom_call" | custom-call | tf_op jit(solution)/shard_map/hand_down/pallas_call | solution.py:71
  108.7 2.8 %collective-permute-start.33 = (bf16[1,256,128]{2,1,0:T(8,128)(2,1)S(1)}, bf16[1,256,128]{2,1,0:T(8,128)(2,1)S(1)}, u32[]{:S(2)}, u32[]{:S(2)}) collective-permute-start(bf16[1,256,128]{2,1,0:T(8,128)(2,1)S(1)} %fusion.8), channel_id=1, source_target_pairs={{0,192},{8,200},{16,208},{24,216},{32,224},{40,232},{48,240},{56,2... | collective-permute-start | bytes 196616 | tf_op jit(solution)/shard_map/ppermute | solution.py:19
  111.5 2.7 %collective-permute-done.24.back_ref = bf16[256,512]{1,0:T(8,128)(2,1)S(1)} collective-permute-done((bf16[256,512]{1,0:T(8,128)(2,1)S(1)}, bf16[256,512]{1,0:T(8,128)(2,1)S(1)}, u32[]{:S(2)}, u32[]{:S(2)}) %collective-permute-start.24) | collective-permute-done | bytes 262176 | tf_op jit(solution)/shard_map/ppermute | solution.py:19
  114.2 2.5 %hand_down.5 = (bf16[256,512]{1,0:T(8,128)(2,1)S(1)}, f32[256,512]{1,0:T(8,128)}) custom-call(s32[1]{0:T(128)} %bitcast.place_ref, bf16[256,512]{1,0:T(8,128)(2,1)S(1)} %collective-permute-done.24.back_ref, bf16[256,512]{1,0:T(8,128)(2,1)} %get-tuple-element.84.rest_ref, f32[256,512]{1,0:T(8,128)} %get-tuple-element.85.refs_0_), custom_call_target="tpu_custom_call" | custom-call | tf_op jit(solution)/shard_map/hand_down/pallas_call | solution.py:71
  117.6 4.3 %collective-permute-done.27.back_ref = bf16[256,512]{1,0:T(8,128)(2,1)S(1)} collective-permute-done((bf16[256,512]{1,0:T(8,128)(2,1)S(1)}, bf16[256,512]{1,0:T(8,128)(2,1)S(1)}, u32[]{:S(2)}, u32[]{:S(2)}) %collective-permute-start.27) | collective-permute-done | bytes 262176 | tf_op jit(solution)/shard_map/ppermute | solution.py:19
  123.9 6.0 %collective-permute-start.30 = (bf16[256,512]{1,0:T(8,128)(2,1)S(1)}, bf16[256,512]{1,0:T(8,128)(2,1)S(1)}, u32[]{:S(2)}, u32[]{:S(2)}) collective-permute-start(bf16[256,512]{1,0:T(8,128)(2,1)S(1)} %get-tuple-element.94), channel_id=1, source_target_pairs={{0,8},{8,0},{16,24},{24,16},{32,40},{40,32},{48,56},{56,48},{64,72... | collective-permute-start | bytes 786440 | tf_op jit(solution)/shard_map/ppermute | solution.py:19
  (123 shorter events, 39.2 us)
Async XLA Ops:
  7.1 7.6 %collective-permute-start.2 = (bf16[256,512]{1,0:T(8,128)(2,1)S(1)}, bf16[256,512]{1,0:T(8,128)(2,1)S(1)}, u32[]{:S(2)}, u32[]{:S(2)}) collective-permute-start(bf16[256,512]{1,0:T(8,128)(2,1)S(1)} %pool_leaf.1.mine_ref), channel_id=1, source_target_pairs={{0,16},{8,24},{16,0},{24,8},{32,48},{40,56},{48,32},{56,40},{64,80... | collective-permute-start | bytes 786440 | tf_op jit(solution)/shard_map/ppermute | solution.py:19
  7.2 11.4 %collective-permute-start.10 = (bf16[256,512]{1,0:T(8,128)(2,1)}, bf16[256,512]{1,0:T(8,128)(2,1)S(1)}, u32[]{:S(2)}, u32[]{:S(2)}) collective-permute-start(bf16[256,512]{1,0:T(8,128)(2,1)} %bitcast.27), channel_id=1, source_target_pairs={{0,1},{1,2},{2,3},{3,4},{4,5},{5,6},{6,7},{7,0},{8,9},{9,10},{10,1... | collective-permute-start | bytes 786440 | tf_op jit(solution)/shard_map/ppermute | solution.py:277
  8.4 10.2 %collective-permute-start.11 = (bf16[256,512]{1,0:T(8,128)(2,1)}, bf16[256,512]{1,0:T(8,128)(2,1)S(1)}, u32[]{:S(2)}, u32[]{:S(2)}) collective-permute-start(bf16[256,512]{1,0:T(8,128)(2,1)} %bitcast.28), channel_id=1, source_target_pairs={{0,7},{1,0},{2,1},{3,2},{4,3},{5,4},{6,5},{7,6},{8,15},{9,8},{10,9... | collective-permute-start | bytes 786440 | tf_op jit(solution)/shard_map/ppermute | solution.py:280
  14.9 7.9 %collective-permute-start.3 = (bf16[256,512]{1,0:T(8,128)(2,1)S(1)}, bf16[256,512]{1,0:T(8,128)(2,1)S(1)}, u32[]{:S(2)}, u32[]{:S(2)}) collective-permute-start(bf16[256,512]{1,0:T(8,128)(2,1)S(1)} %pool_group.3.mine_ref), channel_id=1, source_target_pairs={{0,48},{8,56},{16,32},{24,40},{32,16},{40,24},{48,0},{56,8},{64,11... | collective-permute-start | bytes 786440 | tf_op jit(solution)/shard_map/ppermute | solution.py:19
  18.6 8.2 %collective-permute-start.12 = (bf16[256,512]{1,0:T(8,128)(2,1)S(1)}, bf16[256,512]{1,0:T(8,128)(2,1)S(1)}, u32[]{:S(2)}, u32[]{:S(2)}) collective-permute-start(bf16[256,512]{1,0:T(8,128)(2,1)S(1)} %collective-permute-done.10.refs_1_), channel_id=1, source_target_pairs={{0,1},{1,2},{2,3},{3,4},{4,5},{5,6},{6,7},{7,0},{8,9},{9,10},{10,1... | collective-permute-start | bytes 786440 | tf_op jit(solution)/shard_map/ppermute | solution.py:277
  18.6 8.1 %collective-permute-start.13 = (bf16[256,512]{1,0:T(8,128)(2,1)S(1)}, bf16[256,512]{1,0:T(8,128)(2,1)S(1)}, u32[]{:S(2)}, u32[]{:S(2)}) collective-permute-start(bf16[256,512]{1,0:T(8,128)(2,1)S(1)} %collective-permute-done.11.refs_2_), channel_id=1, source_target_pairs={{0,7},{1,0},{2,1},{3,2},{4,3},{5,4},{6,5},{7,6},{8,15},{9,8},{10,9... | collective-permute-start | bytes 786440 | tf_op jit(solution)/shard_map/ppermute | solution.py:280
  23.0 6.5 %collective-permute-start.4 = (bf16[256,512]{1,0:T(8,128)(2,1)S(1)}, bf16[256,512]{1,0:T(8,128)(2,1)S(1)}, u32[]{:S(2)}, u32[]{:S(2)}) collective-permute-start(bf16[256,512]{1,0:T(8,128)(2,1)S(1)} %pool_group.4.mine_ref), channel_id=1, source_target_pairs={{0,64},{8,72},{16,80},{24,88},{32,96},{40,104},{48,112},{56,120},{... | collective-permute-start | bytes 786440 | tf_op jit(solution)/shard_map/ppermute | solution.py:19
  26.8 6.9 %collective-permute-start.14 = (bf16[256,512]{1,0:T(8,128)(2,1)S(1)}, bf16[256,512]{1,0:T(8,128)(2,1)S(1)}, u32[]{:S(2)}, u32[]{:S(2)}) collective-permute-start(bf16[256,512]{1,0:T(8,128)(2,1)S(1)} %collective-permute-done.12.refs_3_), channel_id=1, source_target_pairs={{0,1},{1,2},{2,3},{3,4},{4,5},{5,6},{6,7},{7,0},{8,9},{9,10},{10,1... | collective-permute-start | bytes 786440 | tf_op jit(solution)/shard_map/ppermute | solution.py:277
  27.3 6.5 %collective-permute-start.15 = (bf16[256,512]{1,0:T(8,128)(2,1)S(1)}, bf16[256,512]{1,0:T(8,128)(2,1)}, u32[]{:S(2)}, u32[]{:S(2)}) collective-permute-start(bf16[256,512]{1,0:T(8,128)(2,1)S(1)} %collective-permute-done.13.refs_4_), channel_id=1, source_target_pairs={{0,7},{1,0},{2,1},{3,2},{4,3},{5,4},{6,5},{7,6},{8,15},{9,8},{10,9... | collective-permute-start | bytes 786440 | tf_op jit(solution)/shard_map/ppermute | solution.py:280
  29.8 6.6 %collective-permute-start.5 = (bf16[256,512]{1,0:T(8,128)(2,1)S(1)}, bf16[256,512]{1,0:T(8,128)(2,1)S(1)}, u32[]{:S(2)}, u32[]{:S(2)}) collective-permute-start(bf16[256,512]{1,0:T(8,128)(2,1)S(1)} %pool_group.5), channel_id=1, source_target_pairs={{0,192},{8,200},{16,208},{24,216},{32,224},{40,232},{48,240},{56,2... | collective-permute-start | bytes 786440 | tf_op jit(solution)/shard_map/ppermute | solution.py:19
  33.7 6.4 %collective-permute-start.16 = (bf16[256,512]{1,0:T(8,128)(2,1)S(1)}, bf16[256,512]{1,0:T(8,128)(2,1)S(1)}, u32[]{:S(2)}, u32[]{:S(2)}) collective-permute-start(bf16[256,512]{1,0:T(8,128)(2,1)S(1)} %collective-permute-done.14.refs_5_), channel_id=1, source_target_pairs={{0,1},{1,2},{2,3},{3,4},{4,5},{5,6},{6,7},{7,0},{8,9},{9,10},{10,1... | collective-permute-start | bytes 786440 | tf_op jit(solution)/shard_map/ppermute | solution.py:277
  46.8 17.8 %collective-permute-start.17 = (bf16[8,256,256]{2,1,0:T(8,128)(2,1)}, bf16[8,256,256]{2,1,0:T(8,128)(2,1)S(1)}, u32[]{:S(2)}, u32[]{:S(2)}) collective-permute-start(bf16[8,256,256]{2,1,0:T(8,128)(2,1)} %get-tuple-element.63), channel_id=1, source_target_pairs={{0,8},{8,0},{16,24},{24,16},{32,40},{40,32},{48,56},{56,48},{64,72... | collective-permute-start | bytes 3145736 | tf_op jit(solution)/shard_map/ppermute | solution.py:19
  79.6 13.7 %collective-permute-start.23 = (bf16[8,256,128]{2,1,0:T(8,128)(2,1)}, bf16[8,256,128]{2,1,0:T(8,128)(2,1)}, u32[]{:S(2)}, u32[]{:S(2)}) collective-permute-start(bf16[8,256,128]{2,1,0:T(8,128)(2,1)} %get-tuple-element.65), channel_id=1, source_target_pairs={{0,16},{8,24},{16,0},{24,8},{32,48},{40,56},{48,32},{56,40},{64,80... | collective-permute-start | bytes 1572872 | tf_op jit(solution)/shard_map/ppermute | solution.py:19
  79.8 20.2 %collective-permute-start.22 = (bf16[8,256,128]{2,1,0:T(8,128)(2,1)}, bf16[8,256,128]{2,1,0:T(8,128)(2,1)S(1)}, u32[]{:S(2)}, u32[]{:S(2)}) collective-permute-start(bf16[8,256,128]{2,1,0:T(8,128)(2,1)} %get-tuple-element.64), channel_id=1, source_target_pairs={{0,64},{8,72},{16,80},{24,88},{32,96},{40,104},{48,112},{56,120},{... | collective-permute-start | bytes 1572872 | tf_op jit(solution)/shard_map/ppermute | solution.py:19
  84.4 12.1 %collective-permute-start.20 = (bf16[256,512]{1,0:T(8,128)(2,1)S(1)}, bf16[256,512]{1,0:T(8,128)(2,1)S(1)}, u32[]{:S(2)}, u32[]{:S(2)}) collective-permute-start(bf16[256,512]{1,0:T(8,128)(2,1)S(1)} %get-tuple-element.72), channel_id=1, source_target_pairs={{0,192},{8,200},{16,208},{24,216},{32,224},{40,232},{48,240},{56,2... | collective-permute-start | bytes 786440 | tf_op jit(solution)/shard_map/ppermute | solution.py:19
  94.4 8.1 %collective-permute-start.26 = (bf16[4,256,128]{2,1,0:T(8,128)(2,1)S(1)}, bf16[4,256,128]{2,1,0:T(8,128)(2,1)S(1)}, u32[]{:S(2)}, u32[]{:S(2)}) collective-permute-start(bf16[4,256,128]{2,1,0:T(8,128)(2,1)S(1)} %get-tuple-element.98), channel_id=1, source_target_pairs={{0,48},{8,56},{16,32},{24,40},{32,16},{40,24},{48,0},{56,8},{64,11... | collective-permute-start | bytes 786440 | tf_op jit(solution)/shard_map/ppermute | solution.py:19
  98.8 6.5 %collective-permute-start.21 = (bf16[256,512]{1,0:T(8,128)(2,1)S(1)}, bf16[256,512]{1,0:T(8,128)(2,1)S(1)}, u32[]{:S(2)}, u32[]{:S(2)}) collective-permute-start(bf16[256,512]{1,0:T(8,128)(2,1)S(1)} %get-tuple-element.74), channel_id=1, source_target_pairs={{0,64},{8,72},{16,80},{24,88},{32,96},{40,104},{48,112},{56,120},{... | collective-permute-start | bytes 786440 | tf_op jit(solution)/shard_map/ppermute | solution.py:19
  100.1 8.5 %collective-permute-start.25 = (bf16[4,256,128]{2,1,0:T(8,128)(2,1)S(1)}, bf16[4,256,128]{2,1,0:T(8,128)(2,1)S(1)}, u32[]{:S(2)}, u32[]{:S(2)}) collective-permute-start(bf16[4,256,128]{2,1,0:T(8,128)(2,1)S(1)} %get-tuple-element.100), channel_id=1, source_target_pairs={{0,192},{8,200},{16,208},{24,216},{32,224},{40,232},{48,240},{56,2... | collective-permute-start | bytes 786440 | tf_op jit(solution)/shard_map/ppermute | solution.py:19
  102.6 6.1 %collective-permute-start.29 = (bf16[2,256,128]{2,1,0:T(8,128)(2,1)S(1)}, bf16[2,256,128]{2,1,0:T(8,128)(2,1)S(1)}, u32[]{:S(2)}, u32[]{:S(2)}) collective-permute-start(bf16[2,256,128]{2,1,0:T(8,128)(2,1)S(1)} %get-tuple-element.102), channel_id=1, source_target_pairs={{0,64},{8,72},{16,80},{24,88},{32,96},{40,104},{48,112},{56,120},{... | collective-permute-start | bytes 393224 | tf_op jit(solution)/shard_map/ppermute | solution.py:19
  107.8 6.4 %collective-permute-start.24 = (bf16[256,512]{1,0:T(8,128)(2,1)S(1)}, bf16[256,512]{1,0:T(8,128)(2,1)S(1)}, u32[]{:S(2)}, u32[]{:S(2)}) collective-permute-start(bf16[256,512]{1,0:T(8,128)(2,1)S(1)} %get-tuple-element.82), channel_id=1, source_target_pairs={{0,48},{8,56},{16,32},{24,40},{32,16},{40,24},{48,0},{56,8},{64,11... | collective-permute-start | bytes 786440 | tf_op jit(solution)/shard_map/ppermute | solution.py:19
  108.6 8.1 %collective-permute-start.28 = (bf16[2,256,128]{2,1,0:T(8,128)(2,1)S(1)}, bf16[2,256,128]{2,1,0:T(8,128)(2,1)S(1)}, u32[]{:S(2)}, u32[]{:S(2)}) collective-permute-start(bf16[2,256,128]{2,1,0:T(8,128)(2,1)S(1)} %get-tuple-element.104), channel_id=1, source_target_pairs={{0,16},{8,24},{16,0},{24,8},{32,48},{40,56},{48,32},{56,40},{64,80... | collective-permute-start | bytes 393224 | tf_op jit(solution)/shard_map/ppermute | solution.py:19
  108.7 8.8 %collective-permute-start.33 = (bf16[1,256,128]{2,1,0:T(8,128)(2,1)S(1)}, bf16[1,256,128]{2,1,0:T(8,128)(2,1)S(1)}, u32[]{:S(2)}, u32[]{:S(2)}) collective-permute-start(bf16[1,256,128]{2,1,0:T(8,128)(2,1)S(1)} %fusion.8), channel_id=1, source_target_pairs={{0,192},{8,200},{16,208},{24,216},{32,224},{40,232},{48,240},{56,2... | collective-permute-start | bytes 196616 | tf_op jit(solution)/shard_map/ppermute | solution.py:19
  116.7 13.1 %collective-permute-start.32 = (bf16[1,256,128]{2,1,0:T(8,128)(2,1)S(1)}, bf16[1,256,128]{2,1,0:T(8,128)(2,1)S(1)}, u32[]{:S(2)}, u32[]{:S(2)}) collective-permute-start(bf16[1,256,128]{2,1,0:T(8,128)(2,1)S(1)} %fusion.9), channel_id=1, source_target_pairs={{0,48},{8,56},{16,32},{24,40},{32,16},{40,24},{48,0},{56,8},{64,11... | collective-permute-start | bytes 196616 | tf_op jit(solution)/shard_map/ppermute | solution.py:19
  123.9 7.2 %collective-permute-start.30 = (bf16[256,512]{1,0:T(8,128)(2,1)S(1)}, bf16[256,512]{1,0:T(8,128)(2,1)S(1)}, u32[]{:S(2)}, u32[]{:S(2)}) collective-permute-start(bf16[256,512]{1,0:T(8,128)(2,1)S(1)} %get-tuple-element.94), channel_id=1, source_target_pairs={{0,8},{8,0},{16,24},{24,16},{32,40},{40,32},{48,56},{56,48},{64,72... | collective-permute-start | bytes 786440 | tf_op jit(solution)/shard_map/ppermute | solution.py:19
  (32 other events, 351.8 us)

commit v2 on v1

--- a/solution.py
+++ b/solution.py
@@ -334,20 +334,6 @@
     offsets = tuple(o for o, _ in ring.blocks)
     full_grad = [b for _, b in ring.blocks]
     col_weight = column_weights(block_doc, my_block, rows, level_count)
-    out_weight = after(out_weight, mine[0][-1])
-    context_grad, send_grad, stacked_grad = pl.pallas_call(
-        functools.partial(context_grad_kernel, offsets),
-        in_specs=[SMEM, SMEM] + [VMEM] * (1 + len(offsets)),
-        out_specs=[VMEM, VMEM, VMEM],
-        out_shape=[
-            jax.ShapeDtypeStruct((rows, features), BF16),
-            jax.ShapeDtypeStruct((len(offsets), rows, features // 2), BF16),
-            jax.ShapeDtypeStruct((len(offsets), rows, features), BF16),
-        ],
-        name="context_grad",
-    )(place, depth, out_weight, *full_grad)
-    other_grad = swapped(send_grad, 0)
-
     slab = pl.BlockSpec((rows, DH), lambda h: (0, h))
     col_slab = pl.BlockSpec((cols, DH), lambda h: (0, h))
     prob_slab = pl.BlockSpec((1, rows, cols), lambda h: (h, 0, 0))
@@ -376,22 +362,20 @@
             )(place, col_weight, queries, keys, other_keys, values, other_values, *mine[i], *other[i])
         )
     contexts = [f[0] for f in forward]
-    (context,) = contexts
-    shape = (seq_count // 4, features // 2, DH)
-    weight_outs = pl.pallas_call(
-        weight_term_kernel,
-        in_specs=[SMEM] + [VMEM] * 4,
-        out_specs=[VMEM] * 4,
-        out_shape=[jax.ShapeDtypeStruct(shape, BF16)] * 4,
-        scratch_shapes=[pltpu.VMEM((features, 2 * rows), BF16)]
-        + [pltpu.VMEM((seq_count // 2, features // 2, DH), BF16)] * 2,
-        name="weight_term",
-    )(place, stacked_grad, other_grad, context, swapped(context, 0))
-    weight_parts = [
-        HalvedSum(weight_outs[0], weight_outs[1], (3, 4, 1, 2)),
-        HalvedSum(weight_outs[2], weight_outs[3], (1, 2, 3, 4)),
-    ]
-    context_grad = after(context_grad, *[w.send for w in weight_parts])
+    out_weight = after(out_weight, contexts[0])
+    context_grad, send_grad, stacked_grad = pl.pallas_call(
+        functools.partial(context_grad_kernel, offsets),
+        in_specs=[SMEM, SMEM] + [VMEM] * (1 + len(offsets)),
+        out_specs=[VMEM, VMEM, VMEM],
+        out_shape=[
+            jax.ShapeDtypeStruct((rows, features), BF16),
+            jax.ShapeDtypeStruct((len(offsets), rows, features // 2), BF16),
+            jax.ShapeDtypeStruct((len(offsets), rows, features), BF16),
+        ],
+        name="context_grad",
+    )(place, depth, out_weight, *full_grad)
+    other_grad = swapped(send_grad, 0)
+
     partial_grads = []
     for i in range(N_PARTS):
         context, prob, kcols, vcols = forward[i]
@@ -425,8 +409,21 @@
             name="hand_down_top",
         )
         back[i] = swapped(send, level_count - 1)
-        for w in weight_parts:
-            w.keep = after(w.keep, send)
+    (context,) = contexts
+    shape = (seq_count // 4, features // 2, DH)
+    weight_outs = pl.pallas_call(
+        weight_term_kernel,
+        in_specs=[SMEM] + [VMEM] * 4,
+        out_specs=[VMEM] * 4,
+        out_shape=[jax.ShapeDtypeStruct(shape, BF16)] * 4,
+        scratch_shapes=[pltpu.VMEM((features, 2 * rows), BF16)]
+        + [pltpu.VMEM((seq_count // 2, features // 2, DH), BF16)] * 2,
+        name="weight_term",
+    )(place, after(stacked_grad, send), other_grad, context, swapped(context, 0))
+    weight_parts = [
+        HalvedSum(weight_outs[0], weight_outs[1], (3, 4, 1, 2)),
+        HalvedSum(weight_outs[2], weight_outs[3], (1, 2, 3, 4)),
+    ]
     for level_num in range(level_count - 2, 0, -1):
         if level_num < level_count - 2:
             for w in weight_parts:

time: 133 us -> 124 us (0.932)
  starting transfers between devices: 47 us -> 40.6 us
  waiting for transfers between devices: 36.4 us -> 33.9 us
    ppermute x27, starting transfers between devices: 34.6 us -> 29.4 us  [swapped(): lax.ppermute(value, 'seq', [(i, i ^ HOPS[level_num]) for i in range(count)])]
    ppermute x4, waiting for transfers between devices: 11.2 us -> 6.05 us  [step(): lax.ppermute(self.below, self.axis, [(i, (i + 1) % count) for i in range(...]
    ppermute x27, waiting for transfers between devices: 25.2 us -> 27.9 us  [swapped(): lax.ppermute(value, 'seq', [(i, i ^ HOPS[level_num]) for i in range(count)])]
    ppermute x4, starting transfers between devices: 3.17 us -> 1.79 us  [step(): lax.ppermute(self.below, self.axis, [(i, (i + 1) % count) for i in range(...]
  transfers between devices with their start and end apart: 34 -> 34, of which waited for: 19 -> 15; matrix products, arithmetic and copies ran while one was open for 4% -> 4% of each run, Pallas kernels for 15% -> 16%
where the time goes in v2:
time: 124 us
  starting transfers between devices  40.6 us (33%)
  Pallas kernels  40 us (32%)
  waiting for transfers between devices  33.9 us (27%)
  other arithmetic  5.08 us (4%)
  local copies, waits for them, and re-layouts  3.23 us (3%)
    ppermute x27, starting transfers between devices, swapped(): lax.ppermute(value, 'seq', [(i, i ^ HOPS[level_num]) for i in range(count)])  29.4 us
    ppermute x27, waiting for transfers between devices, swapped(): lax.ppermute(value, 'seq', [(i, i ^ HOPS[level_num]) for i in range(count)])  27.9 us
    pallas_call x9, Pallas kernels, near_call(): pl.pallas_call(kernel, in_specs=[SMEM] + [VMEM] * (len(near) + len(far)),...  13.4 us
    ppermute x3, starting transfers between devices, step(): lax.ppermute(self.above, self.axis, [(i, (i - 1) % count) for i in range(...  9.37 us
    pallas_call x1, Pallas kernels, local(): pl.pallas_call(functools.partial(backward_kernel, scaling, n_up), grid=(p...  7.49 us
    pallas_call x1, Pallas kernels, local(): pl.pallas_call(functools.partial(forward_kernel, scaling, n_up), grid=(pa...  7.17 us
    ppermute x4, waiting for transfers between devices, step(): lax.ppermute(self.below, self.axis, [(i, (i + 1) % count) for i in range(...  6.05 us
    pallas_call x1, Pallas kernels, local(): pl.pallas_call(weight_term_kernel, in_specs=[SMEM] + [VMEM] * 4, out_spec...  6.02 us
  transfers between devices with their start and end apart: 34, of which 15 were waited for; matrix products, arithmetic and copies ran while one was open for 4% of the time, Pallas kernels for 16%

profile of v2, /device:TPU:1, one launch (start us, length us, event | category | flops | bytes accessed | tf_op | source)
XLA Modules:
  0.0 123.8 jit_solution(3491554075547146729)
XLA Ops:
  0.7 3.3 %collective-permute-start.1 = (bf16[256,512]{1,0:T(8,128)(2,1)}, bf16[256,512]{1,0:T(8,128)(2,1)S(1)}, u32[]{:S(2)}, u32[]{:S(2)}) collective-permute-start(bf16[256,512]{1,0:T(8,128)(2,1)} %bitcast.24), channel_id=1, source_target_pairs={{0,8},{8,0},{16,24},{24,16},{32,40},{40,32},{48,56},{56,48},{64,72... | collective-permute-start | bytes 786440 | tf_op jit(solution)/shard_map/ppermute | solution.py:19
  8.4 3.9 %collective-permute-start.11 = (bf16[256,512]{1,0:T(8,128)(2,1)}, bf16[256,512]{1,0:T(8,128)(2,1)S(1)}, u32[]{:S(2)}, u32[]{:S(2)}) collective-permute-start(bf16[256,512]{1,0:T(8,128)(2,1)} %bitcast.28), channel_id=1, source_target_pairs={{0,7},{1,0},{2,1},{3,2},{4,3},{5,4},{6,5},{7,6},{8,15},{9,8},{10,9... | collective-permute-start | bytes 786440 | tf_op jit(solution)/shard_map/ppermute | solution.py:280
  12.3 2.4 %collective-permute-done.2.other_ref.refs_4_ = bf16[256,512]{1,0:T(8,128)(2,1)S(1)} collective-permute-done((bf16[256,512]{1,0:T(8,128)(2,1)S(1)}, bf16[256,512]{1,0:T(8,128)(2,1)S(1)}, u32[]{:S(2)}, u32[]{:S(2)}) %collective-permute-start.2) | collective-permute-done | bytes 262176 | tf_op jit(solution)/shard_map/ppermute | solution.py:19
  16.0 2.6 %collective-permute-done.10.refs_1_ = bf16[256,512]{1,0:T(8,128)(2,1)S(1)} collective-permute-done((bf16[256,512]{1,0:T(8,128)(2,1)}, bf16[256,512]{1,0:T(8,128)(2,1)S(1)}, u32[]{:S(2)}, u32[]{:S(2)}) %collective-permute-start.10) | collective-permute-done | bytes 262176 | tf_op jit(solution)/shard_map/ppermute | solution.py:277
  18.7 3.1 %collective-permute-start.13 = (bf16[256,512]{1,0:T(8,128)(2,1)S(1)}, bf16[256,512]{1,0:T(8,128)(2,1)S(1)}, u32[]{:S(2)}, u32[]{:S(2)}) collective-permute-start(bf16[256,512]{1,0:T(8,128)(2,1)S(1)} %collective-permute-done.11.refs_2_), channel_id=1, source_target_pairs={{0,7},{1,0},{2,1},{3,2},{4,3},{5,4},{6,5},{7,6},{8,15},{9,8},{10,9... | collective-permute-start | bytes 786440 | tf_op jit(solution)/shard_map/ppermute | solution.py:280
  23.3 3.5 %collective-permute-done.12.refs_3_ = bf16[256,512]{1,0:T(8,128)(2,1)S(1)} collective-permute-done((bf16[256,512]{1,0:T(8,128)(2,1)S(1)}, bf16[256,512]{1,0:T(8,128)(2,1)S(1)}, u32[]{:S(2)}, u32[]{:S(2)}) %collective-permute-start.12) | collective-permute-done | bytes 262176 | tf_op jit(solution)/shard_map/ppermute | solution.py:277
  27.3 2.3 %collective-permute-start.15 = (bf16[256,512]{1,0:T(8,128)(2,1)S(1)}, bf16[256,512]{1,0:T(8,128)(2,1)}, u32[]{:S(2)}, u32[]{:S(2)}) collective-permute-start(bf16[256,512]{1,0:T(8,128)(2,1)S(1)} %collective-permute-done.13.refs_4_), channel_id=1, source_target_pairs={{0,7},{1,0},{2,1},{3,2},{4,3},{5,4},{6,5},{7,6},{8,15},{9,8},{10,9... | collective-permute-start | bytes 786440 | tf_op jit(solution)/shard_map/ppermute | solution.py:280
  29.8 2.6 %collective-permute-start.5 = (bf16[256,512]{1,0:T(8,128)(2,1)S(1)}, bf16[256,512]{1,0:T(8,128)(2,1)S(1)}, u32[]{:S(2)}, u32[]{:S(2)}) collective-permute-start(bf16[256,512]{1,0:T(8,128)(2,1)S(1)} %pool_group.5), channel_id=1, source_target_pairs={{0,192},{8,200},{16,208},{24,216},{32,224},{40,232},{48,240},{56,2... | collective-permute-start | bytes 786440 | tf_op jit(solution)/shard_map/ppermute | solution.py:19
  32.5 3.1 %collective-permute-start.6 = (bf16[256,512]{1,0:T(8,128)(2,1)S(1)}, bf16[256,512]{1,0:T(8,128)(2,1)S(1)}, u32[]{:S(2)}, u32[]{:S(2)}) collective-permute-start(bf16[256,512]{1,0:T(8,128)(2,1)S(1)} %collective-permute-done.2.other_ref.refs_4_), channel_id=1, source_target_pairs={{0,8},{8,0},{16,24},{24,16},{32,40},{40,32},{48,56},{56,48},{64,72... | collective-permute-start | bytes 786440 | tf_op jit(solution)/shard_map/ppermute | solution.py:19
  35.8 3.3 %collective-permute-start.8 = (bf16[256,512]{1,0:T(8,128)(2,1)S(1)}, bf16[256,512]{1,0:T(8,128)(2,1)S(1)}, u32[]{:S(2)}, u32[]{:S(2)}) collective-permute-start(bf16[256,512]{1,0:T(8,128)(2,1)S(1)} %collective-permute-done.4.other_ref.refs_6_), channel_id=1, source_target_pairs={{0,8},{8,0},{16,24},{24,16},{32,40},{40,32},{48,56},{56,48},{64,72... | collective-permute-start | bytes 786440 | tf_op jit(solution)/shard_map/ppermute | solution.py:19
  43.0 7.2 %attention_forward.1 = (bf16[256,512]{1,0:T(8,128)(2,1)}, bf16[4,256,1536]{2,1,0:T(8,128)(2,1)}, bf16[1536,512]{1,0:T(8,128)(2,1)}, bf16[1536,512]{1,0:T(8,128)(2,1)}) custom-call(s32[1]{0:T(128)} %bitcast.place_ref, f32[1,1536]{1,0:T(1,128)} %select_n.33.weight_ref, bf16[256,512]{1,0:T(8,128)(2,1)} %bitcast.18, bf16[256,512]{1,0:T(8,128)(2,1)} %bitcast.23, ...), custom_call_target="tpu_custom_call" | custom-call | tf_op jit(solution)/shard_map/attention_forward/pallas_call | solution.py:348
  50.3 5.9 %context_grad.1 = (bf16[256,512]{1,0:T(8,128)(2,1)}, bf16[8,256,256]{2,1,0:T(8,128)(2,1)}, bf16[8,256,512]{2,1,0:T(8,128)(2,1)}) custom-call(s32[1]{0:T(128)} %bitcast.place_ref, s32[1]{0:T(128)} %bitcast.6.depth_ref, bf16[512,4096]{1,0:T(8,128)(2,1)} %weight_ref, bf16[256,512]{1,0:T(8,128)(2,1)} %bitcast.29, bf16[256,512]{1,0:T(8,128)(2,1)} %copy-done.14, ...), custom_call_target="tpu_custom_call" | custom-call | tf_op jit(solution)/shard_map/context_grad/pallas_call | solution.py:366
  56.2 7.5 %attention_backward.1 = (bf16[256,512]{1,0:T(8,128)(2,1)}, bf16[256,512]{1,0:T(8,128)(2,1)}, bf16[256,512]{1,0:T(8,128)(2,1)}, bf16[256,512]{1,0:T(8,128)(2,1)},...) custom-call(s32[1]{0:T(128)} %bitcast.place_ref, bf16[256,512]{1,0:T(8,128)(2,1)} %bitcast.19, ...), custom_call_target="tpu_custom_call" | custom-call | tf_op jit(solution)/shard_map/attention_backward/pallas_call | solution.py:383
  64.4 2.3 %collective-permute-done.17.recv_ref = bf16[4,256,512]{2,1,0:T(8,128)(2,1)S(1)} collective-permute-done((bf16[4,256,512]{2,1,0:T(8,128)(2,1)}, bf16[4,256,512]{2,1,0:T(8,128)(2,1)S(1)}, u32[]{:S(2)}, u32[]{:S(2)}) %collective-permute-start.17) | collective-permute-done | bytes 1048608 | tf_op jit(solution)/shard_map/ppermute | solution.py:19
  70.5 6.0 %weight_term.1 = (bf16[8,256,128]{2,1,0:T(8,128)(2,1)}, bf16[8,256,128]{2,1,0:T(8,128)(2,1)}, bf16[8,256,128]{2,1,0:T(8,128)(2,1)}, bf16[8,256,128]{2,1,0:T(8,128)(2,1)}) custom-call(s32[1]{0:T(128)} %bitcast.place_ref, bf16[8,256,512]{2,1,0:T(8,128)(2,1)} %get-tuple-element.69.full_ref, bf16[8,256,256]{2,1,0:T(8,128)(2,1)} %copy-done.6, ...), custom_call_target="tpu_custom_call" | custom-call | tf_op jit(solution)/shard_map/weight_term/pallas_call | solution.py:414
  79.2 6.2 %collective-permute-done.18.back_ref = bf16[256,512]{1,0:T(8,128)(2,1)S(1)} collective-permute-done((bf16[256,512]{1,0:T(8,128)(2,1)S(1)}, bf16[256,512]{1,0:T(8,128)(2,1)S(1)}, u32[]{:S(2)}, u32[]{:S(2)}) %collective-permute-start.18) | collective-permute-done | bytes 262176 | tf_op jit(solution)/shard_map/ppermute | solution.py:19
  85.4 2.3 %hand_down.3 = (bf16[256,512]{1,0:T(8,128)(2,1)S(1)}, f32[256,512]{1,0:T(8,128)}) custom-call(s32[1]{0:T(128)} %bitcast.place_ref, bf16[256,512]{1,0:T(8,128)(2,1)S(1)} %collective-permute-done.18.back_ref, bf16[256,512]{1,0:T(8,128)(2,1)} %get-tuple-element.66.rest_ref), custom_call_target="tpu_custom_call" | custom-call | tf_op jit(solution)/shard_map/hand_down/pallas_call | solution.py:71
  91.4 2.6 %collective-permute-start.25 = (bf16[4,256,128]{2,1,0:T(8,128)(2,1)S(1)}, bf16[4,256,128]{2,1,0:T(8,128)(2,1)S(1)}, u32[]{:S(2)}, u32[]{:S(2)}) collective-permute-start(bf16[4,256,128]{2,1,0:T(8,128)(2,1)S(1)} %get-tuple-element.96), channel_id=1, source_target_pairs={{0,192},{8,200},{16,208},{24,216},{32,224},{40,232},{48,240},{56,2... | collective-permute-start | bytes 786440 | tf_op jit(solution)/shard_map/ppermute | solution.py:19
  95.7 2.5 %hand_down.4 = (bf16[256,512]{1,0:T(8,128)(2,1)S(1)}, f32[256,512]{1,0:T(8,128)}) custom-call(s32[1]{0:T(128)} %bitcast.place_ref, bf16[256,512]{1,0:T(8,128)(2,1)S(1)} %collective-permute-done.19.back_ref, bf16[256,512]{1,0:T(8,128)(2,1)} %get-tuple-element.76.rest_ref, f32[256,512]{1,0:T(8,128)} %get-tuple-element.77.refs_0_), custom_call_target="tpu_custom_call" | custom-call | tf_op jit(solution)/shard_map/hand_down/pallas_call | solution.py:71
  99.5 2.5 %collective-permute-done.26 = bf16[4,256,128]{2,1,0:T(8,128)(2,1)S(1)} collective-permute-done((bf16[4,256,128]{2,1,0:T(8,128)(2,1)S(1)}, bf16[4,256,128]{2,1,0:T(8,128)(2,1)S(1)}, u32[]{:S(2)}, u32[]{:S(2)}) %collective-permute-start.26) | collective-permute-done | bytes 262176 | tf_op jit(solution)/shard_map/ppermute | solution.py:19
  102.4 5.4 %collective-permute-done.24.back_ref = bf16[256,512]{1,0:T(8,128)(2,1)S(1)} collective-permute-done((bf16[256,512]{1,0:T(8,128)(2,1)S(1)}, bf16[256,512]{1,0:T(8,128)(2,1)S(1)}, u32[]{:S(2)}, u32[]{:S(2)}) %collective-permute-start.24) | collective-permute-done | bytes 262176 | tf_op jit(solution)/shard_map/ppermute | solution.py:19
  107.8 2.5 %hand_down.5 = (bf16[256,512]{1,0:T(8,128)(2,1)S(1)}, f32[256,512]{1,0:T(8,128)}) custom-call(s32[1]{0:T(128)} %bitcast.place_ref, bf16[256,512]{1,0:T(8,128)(2,1)S(1)} %collective-permute-done.24.back_ref, bf16[256,512]{1,0:T(8,128)(2,1)} %get-tuple-element.80.rest_ref, f32[256,512]{1,0:T(8,128)} %get-tuple-element.81.refs_0_), custom_call_target="tpu_custom_call" | custom-call | tf_op jit(solution)/shard_map/hand_down/pallas_call | solution.py:71
  111.9 2.8 %collective-permute-done.32 = bf16[1,256,128]{2,1,0:T(8,128)(2,1)S(1)} collective-permute-done((bf16[1,256,128]{2,1,0:T(8,128)(2,1)S(1)}, bf16[1,256,128]{2,1,0:T(8,128)(2,1)S(1)}, u32[]{:S(2)}, u32[]{:S(2)}) %collective-permute-start.32) | collective-permute-done | bytes 65568 | tf_op jit(solution)/shard_map/ppermute | solution.py:19
  118.1 3.0 %collective-permute-start.31 = (bf16[256,512]{1,0:T(8,128)(2,1)S(1)}, bf16[256,512]{1,0:T(8,128)(2,1)S(1)}, u32[]{:S(2)}, u32[]{:S(2)}) collective-permute-start(bf16[256,512]{1,0:T(8,128)(2,1)S(1)} %get-tuple-element.92), channel_id=1, source_target_pairs={{0,8},{8,0},{16,24},{24,16},{32,40},{40,32},{48,56},{56,48},{64,72... | collective-permute-start | bytes 786440 | tf_op jit(solution)/shard_map/ppermute | solution.py:19
  (119 shorter events, 34.2 us)
Async XLA Ops:
  7.1 7.6 %collective-permute-start.2 = (bf16[256,512]{1,0:T(8,128)(2,1)S(1)}, bf16[256,512]{1,0:T(8,128)(2,1)S(1)}, u32[]{:S(2)}, u32[]{:S(2)}) collective-permute-start(bf16[256,512]{1,0:T(8,128)(2,1)S(1)} %pool_leaf.1.mine_ref), channel_id=1, source_target_pairs={{0,16},{8,24},{16,0},{24,8},{32,48},{40,56},{48,32},{56,40},{64,80... | collective-permute-start | bytes 786440 | tf_op jit(solution)/shard_map/ppermute | solution.py:19
  7.2 11.4 %collective-permute-start.10 = (bf16[256,512]{1,0:T(8,128)(2,1)}, bf16[256,512]{1,0:T(8,128)(2,1)S(1)}, u32[]{:S(2)}, u32[]{:S(2)}) collective-permute-start(bf16[256,512]{1,0:T(8,128)(2,1)} %bitcast.27), channel_id=1, source_target_pairs={{0,1},{1,2},{2,3},{3,4},{4,5},{5,6},{6,7},{7,0},{8,9},{9,10},{10,1... | collective-permute-start | bytes 786440 | tf_op jit(solution)/shard_map/ppermute | solution.py:277
  8.4 10.2 %collective-permute-start.11 = (bf16[256,512]{1,0:T(8,128)(2,1)}, bf16[256,512]{1,0:T(8,128)(2,1)S(1)}, u32[]{:S(2)}, u32[]{:S(2)}) collective-permute-start(bf16[256,512]{1,0:T(8,128)(2,1)} %bitcast.28), channel_id=1, source_target_pairs={{0,7},{1,0},{2,1},{3,2},{4,3},{5,4},{6,5},{7,6},{8,15},{9,8},{10,9... | collective-permute-start | bytes 786440 | tf_op jit(solution)/shard_map/ppermute | solution.py:280
  14.9 7.9 %collective-permute-start.3 = (bf16[256,512]{1,0:T(8,128)(2,1)S(1)}, bf16[256,512]{1,0:T(8,128)(2,1)S(1)}, u32[]{:S(2)}, u32[]{:S(2)}) collective-permute-start(bf16[256,512]{1,0:T(8,128)(2,1)S(1)} %pool_group.3.mine_ref), channel_id=1, source_target_pairs={{0,48},{8,56},{16,32},{24,40},{32,16},{40,24},{48,0},{56,8},{64,11... | collective-permute-start | bytes 786440 | tf_op jit(solution)/shard_map/ppermute | solution.py:19
  18.6 8.2 %collective-permute-start.12 = (bf16[256,512]{1,0:T(8,128)(2,1)S(1)}, bf16[256,512]{1,0:T(8,128)(2,1)S(1)}, u32[]{:S(2)}, u32[]{:S(2)}) collective-permute-start(bf16[256,512]{1,0:T(8,128)(2,1)S(1)} %collective-permute-done.10.refs_1_), channel_id=1, source_target_pairs={{0,1},{1,2},{2,3},{3,4},{4,5},{5,6},{6,7},{7,0},{8,9},{9,10},{10,1... | collective-permute-start | bytes 786440 | tf_op jit(solution)/shard_map/ppermute | solution.py:277
  18.7 8.2 %collective-permute-start.13 = (bf16[256,512]{1,0:T(8,128)(2,1)S(1)}, bf16[256,512]{1,0:T(8,128)(2,1)S(1)}, u32[]{:S(2)}, u32[]{:S(2)}) collective-permute-start(bf16[256,512]{1,0:T(8,128)(2,1)S(1)} %collective-permute-done.11.refs_2_), channel_id=1, source_target_pairs={{0,7},{1,0},{2,1},{3,2},{4,3},{5,4},{6,5},{7,6},{8,15},{9,8},{10,9... | collective-permute-start | bytes 786440 | tf_op jit(solution)/shard_map/ppermute | solution.py:280
  23.0 6.6 %collective-permute-start.4 = (bf16[256,512]{1,0:T(8,128)(2,1)S(1)}, bf16[256,512]{1,0:T(8,128)(2,1)S(1)}, u32[]{:S(2)}, u32[]{:S(2)}) collective-permute-start(bf16[256,512]{1,0:T(8,128)(2,1)S(1)} %pool_group.4.mine_ref), channel_id=1, source_target_pairs={{0,64},{8,72},{16,80},{24,88},{32,96},{40,104},{48,112},{56,120},{... | collective-permute-start | bytes 786440 | tf_op jit(solution)/shard_map/ppermute | solution.py:19
  26.8 8.8 %collective-permute-start.14 = (bf16[256,512]{1,0:T(8,128)(2,1)S(1)}, bf16[256,512]{1,0:T(8,128)(2,1)}, u32[]{:S(2)}, u32[]{:S(2)}) collective-permute-start(bf16[256,512]{1,0:T(8,128)(2,1)S(1)} %collective-permute-done.12.refs_3_), channel_id=1, source_target_pairs={{0,1},{1,2},{2,3},{3,4},{4,5},{5,6},{6,7},{7,0},{8,9},{9,10},{10,1... | collective-permute-start | bytes 786440 | tf_op jit(solution)/shard_map/ppermute | solution.py:277
  27.3 8.4 %collective-permute-start.15 = (bf16[256,512]{1,0:T(8,128)(2,1)S(1)}, bf16[256,512]{1,0:T(8,128)(2,1)}, u32[]{:S(2)}, u32[]{:S(2)}) collective-permute-start(bf16[256,512]{1,0:T(8,128)(2,1)S(1)} %collective-permute-done.13.refs_4_), channel_id=1, source_target_pairs={{0,7},{1,0},{2,1},{3,2},{4,3},{5,4},{6,5},{7,6},{8,15},{9,8},{10,9... | collective-permute-start | bytes 786440 | tf_op jit(solution)/shard_map/ppermute | solution.py:280
  29.8 9.3 %collective-permute-start.5 = (bf16[256,512]{1,0:T(8,128)(2,1)S(1)}, bf16[256,512]{1,0:T(8,128)(2,1)S(1)}, u32[]{:S(2)}, u32[]{:S(2)}) collective-permute-start(bf16[256,512]{1,0:T(8,128)(2,1)S(1)} %pool_group.5), channel_id=1, source_target_pairs={{0,192},{8,200},{16,208},{24,216},{32,224},{40,232},{48,240},{56,2... | collective-permute-start | bytes 786440 | tf_op jit(solution)/shard_map/ppermute | solution.py:19
  32.5 9.6 %collective-permute-start.6 = (bf16[256,512]{1,0:T(8,128)(2,1)S(1)}, bf16[256,512]{1,0:T(8,128)(2,1)S(1)}, u32[]{:S(2)}, u32[]{:S(2)}) collective-permute-start(bf16[256,512]{1,0:T(8,128)(2,1)S(1)} %collective-permute-done.2.other_ref.refs_4_), channel_id=1, source_target_pairs={{0,8},{8,0},{16,24},{24,16},{32,40},{40,32},{48,56},{56,48},{64,72... | collective-permute-start | bytes 786440 | tf_op jit(solution)/shard_map/ppermute | solution.py:19
  35.6 6.5 %collective-permute-start.7 = (bf16[256,512]{1,0:T(8,128)(2,1)S(1)}, bf16[256,512]{1,0:T(8,128)(2,1)S(1)}, u32[]{:S(2)}, u32[]{:S(2)}) collective-permute-start(bf16[256,512]{1,0:T(8,128)(2,1)S(1)} %collective-permute-done.3.other_ref.refs_5_), channel_id=1, source_target_pairs={{0,8},{8,0},{16,24},{24,16},{32,40},{40,32},{48,56},{56,48},{64,72... | collective-permute-start | bytes 786440 | tf_op jit(solution)/shard_map/ppermute | solution.py:19
  35.7 14.6 %collective-permute-start.16 = (bf16[256,512]{1,0:T(8,128)(2,1)}, bf16[256,512]{1,0:T(8,128)(2,1)}, u32[]{:S(2)}, u32[]{:S(2)}) collective-permute-start(bf16[256,512]{1,0:T(8,128)(2,1)} %collective-permute-done.14.refs_5_), channel_id=1, source_target_pairs={{0,1},{1,2},{2,3},{3,4},{4,5},{5,6},{6,7},{7,0},{8,9},{9,10},{10,1... | collective-permute-start | bytes 786440 | tf_op jit(solution)/shard_map/ppermute | solution.py:277
  35.8 6.3 %collective-permute-start.8 = (bf16[256,512]{1,0:T(8,128)(2,1)S(1)}, bf16[256,512]{1,0:T(8,128)(2,1)S(1)}, u32[]{:S(2)}, u32[]{:S(2)}) collective-permute-start(bf16[256,512]{1,0:T(8,128)(2,1)S(1)} %collective-permute-done.4.other_ref.refs_6_), channel_id=1, source_target_pairs={{0,8},{8,0},{16,24},{24,16},{32,40},{40,32},{48,56},{56,48},{64,72... | collective-permute-start | bytes 786440 | tf_op jit(solution)/shard_map/ppermute | solution.py:19
  76.5 13.7 %collective-permute-start.22 = (bf16[8,256,128]{2,1,0:T(8,128)(2,1)}, bf16[8,256,128]{2,1,0:T(8,128)(2,1)S(1)}, u32[]{:S(2)}, u32[]{:S(2)}) collective-permute-start(bf16[8,256,128]{2,1,0:T(8,128)(2,1)} %get-tuple-element.72), channel_id=1, source_target_pairs={{0,64},{8,72},{16,80},{24,88},{32,96},{40,104},{48,112},{56,120},{... | collective-permute-start | bytes 1572872 | tf_op jit(solution)/shard_map/ppermute | solution.py:19
  76.9 17.0 %collective-permute-start.23 = (bf16[8,256,128]{2,1,0:T(8,128)(2,1)}, bf16[8,256,128]{2,1,0:T(8,128)(2,1)S(1)}, u32[]{:S(2)}, u32[]{:S(2)}) collective-permute-start(bf16[8,256,128]{2,1,0:T(8,128)(2,1)} %get-tuple-element.74), channel_id=1, source_target_pairs={{0,16},{8,24},{16,0},{24,8},{32,48},{40,56},{48,32},{56,40},{64,80... | collective-permute-start | bytes 1572872 | tf_op jit(solution)/shard_map/ppermute | solution.py:19
  76.9 8.4 %collective-permute-start.18 = (bf16[256,512]{1,0:T(8,128)(2,1)S(1)}, bf16[256,512]{1,0:T(8,128)(2,1)S(1)}, u32[]{:S(2)}, u32[]{:S(2)}) collective-permute-start(bf16[256,512]{1,0:T(8,128)(2,1)S(1)} %get-tuple-element.65), channel_id=1, source_target_pairs={{0,192},{8,200},{16,208},{24,216},{32,224},{40,232},{48,240},{56,2... | collective-permute-start | bytes 786440 | tf_op jit(solution)/shard_map/ppermute | solution.py:19
  87.7 8.0 %collective-permute-start.19 = (bf16[256,512]{1,0:T(8,128)(2,1)S(1)}, bf16[256,512]{1,0:T(8,128)(2,1)S(1)}, u32[]{:S(2)}, u32[]{:S(2)}) collective-permute-start(bf16[256,512]{1,0:T(8,128)(2,1)S(1)} %get-tuple-element.67), channel_id=1, source_target_pairs={{0,64},{8,72},{16,80},{24,88},{32,96},{40,104},{48,112},{56,120},{... | collective-permute-start | bytes 786440 | tf_op jit(solution)/shard_map/ppermute | solution.py:19
  91.4 8.0 %collective-permute-start.25 = (bf16[4,256,128]{2,1,0:T(8,128)(2,1)S(1)}, bf16[4,256,128]{2,1,0:T(8,128)(2,1)S(1)}, u32[]{:S(2)}, u32[]{:S(2)}) collective-permute-start(bf16[4,256,128]{2,1,0:T(8,128)(2,1)S(1)} %get-tuple-element.96), channel_id=1, source_target_pairs={{0,192},{8,200},{16,208},{24,216},{32,224},{40,232},{48,240},{56,2... | collective-permute-start | bytes 786440 | tf_op jit(solution)/shard_map/ppermute | solution.py:19
  94.1 7.9 %collective-permute-start.26 = (bf16[4,256,128]{2,1,0:T(8,128)(2,1)S(1)}, bf16[4,256,128]{2,1,0:T(8,128)(2,1)S(1)}, u32[]{:S(2)}, u32[]{:S(2)}) collective-permute-start(bf16[4,256,128]{2,1,0:T(8,128)(2,1)S(1)} %get-tuple-element.94), channel_id=1, source_target_pairs={{0,48},{8,56},{16,32},{24,40},{32,16},{40,24},{48,0},{56,8},{64,11... | collective-permute-start | bytes 786440 | tf_op jit(solution)/shard_map/ppermute | solution.py:19
  98.2 9.6 %collective-permute-start.24 = (bf16[256,512]{1,0:T(8,128)(2,1)S(1)}, bf16[256,512]{1,0:T(8,128)(2,1)S(1)}, u32[]{:S(2)}, u32[]{:S(2)}) collective-permute-start(bf16[256,512]{1,0:T(8,128)(2,1)S(1)} %get-tuple-element.78), channel_id=1, source_target_pairs={{0,48},{8,56},{16,32},{24,40},{32,16},{40,24},{48,0},{56,8},{64,11... | collective-permute-start | bytes 786440 | tf_op jit(solution)/shard_map/ppermute | solution.py:19
  99.4 10.8 %collective-permute-start.28 = (bf16[2,256,128]{2,1,0:T(8,128)(2,1)S(1)}, bf16[2,256,128]{2,1,0:T(8,128)(2,1)S(1)}, u32[]{:S(2)}, u32[]{:S(2)}) collective-permute-start(bf16[2,256,128]{2,1,0:T(8,128)(2,1)S(1)} %get-tuple-element.100), channel_id=1, source_target_pairs={{0,16},{8,24},{16,0},{24,8},{32,48},{40,56},{48,32},{56,40},{64,80... | collective-permute-start | bytes 393224 | tf_op jit(solution)/shard_map/ppermute | solution.py:19
  102.1 9.7 %collective-permute-start.29 = (bf16[2,256,128]{2,1,0:T(8,128)(2,1)S(1)}, bf16[2,256,128]{2,1,0:T(8,128)(2,1)S(1)}, u32[]{:S(2)}, u32[]{:S(2)}) collective-permute-start(bf16[2,256,128]{2,1,0:T(8,128)(2,1)S(1)} %get-tuple-element.98), channel_id=1, source_target_pairs={{0,64},{8,72},{16,80},{24,88},{32,96},{40,104},{48,112},{56,120},{... | collective-permute-start | bytes 393224 | tf_op jit(solution)/shard_map/ppermute | solution.py:19
  111.8 9.3 %collective-permute-start.33 = (bf16[1,256,128]{2,1,0:T(8,128)(2,1)S(1)}, bf16[1,256,128]{2,1,0:T(8,128)(2,1)S(1)}, u32[]{:S(2)}, u32[]{:S(2)}) collective-permute-start(bf16[1,256,128]{2,1,0:T(8,128)(2,1)S(1)} %fusion.8), channel_id=1, source_target_pairs={{0,192},{8,200},{16,208},{24,216},{32,224},{40,232},{48,240},{56,2... | collective-permute-start | bytes 196616 | tf_op jit(solution)/shard_map/ppermute | solution.py:19
  (30 other events, 371.9 us)
